TPU v7x, 32 devices: a whole 2x2x4 slice. The times are simulated.
32 devices in a mesh: gx: 4 (over x, core), gy: 8 (over z, y).
Axes of the slice: x: 2, y: 2, z: 4, core: 2. Of those that a mesh axis runs over, the one named last changes fastest.
Arguments:
- blocks: float32 [8, 8, 9, 128, 128], P('gx', 'gy'), may hold values from -0.0625 to 0.0625
- pair_mask: int32 [8, 8, 9, 8, 8], P('gx', 'gy'), may hold values 0 or 1
- rhs_rows: float32 [8, 8, 9, 128, 128], P('gx', 'gy'), may hold values from -6 to 6
- counts: int32 [8, 8, 8], P('gx', 'gy'), may hold values from 1 to 3, as said below
Outputs:
- solution: float32 [8, 8, 9, 128, 128], P('gx', 'gy')
Inputs may be any that keep to these rules, and one draw needn't show every extreme that they name: `counts`: cut the first block index into runs of 2 blocks. Within each second index b, run a and run a + 2 together hold at most 2 blocks that have an atom with a count of 2 or more, and some run holds 2 such blocks; at least one atom takes 3 iterations and at least one takes 1.
All inputs are finite; a program needn't handle non-finite values. No bound on the sum of `pair_mask` on one device may be relied on, other than what follows from the above.
Results may differ from a plain program's by a relative error of at most 0.0003.
Values sent between devices are 32-bit elements; how exact they have to be, the bound alone decides.
A program may use at most 128 MiB of HBM per device.

v0:
```python
import functools

import jax
import jax.numpy as jnp
from jax import lax
from jax.experimental import pallas as pl
from jax.experimental.pallas import tpu as pltpu
from jax.sharding import PartitionSpec as P

ITERS = 3
MESH = pl.DeviceIdType.MESH
F32 = jnp.float32
BF16 = jnp.bfloat16
CHUNK = 64


def guarded(top, bottom, floor_val):
    return top * bottom / (bottom * bottom + floor_val * floor_val)


def split(value):
    high = value.astype(BF16)
    return high, (value - high.astype(F32)).astype(BF16)


def kernel(
    blocks, masks, rhs, limits, own_masks, out,
    own_c, gy_c, gx_c, dg_c, gy_m, gx_m, dg_m, gy_r,
    mid, edge, v_hi, v_lo, res,
    shadow, w_vec, y_first, y_second, u_first, u_second, vec, direc, sol,
    send_sem, recv_sem, local_sem,
):
    b = blocks.shape[-1]
    atoms = masks.shape[-1]
    orb = b // atoms
    strip = 3 * b
    rows = 9 * b
    gx, gy = lax.axis_index("gx"), lax.axis_index("gy")
    ngx, ngy = lax.axis_size("gx"), lax.axis_size("gy")
    gx_to = (gx < ngx - 1, gx > 0)
    gx_from = (gx > 0, gx < ngx - 1)
    gy_to = (gy < ngy - 1, gy > 0)
    gy_from = (gy > 0, gy < ngy - 1)
    gx_dev = ((gx + 1, gy), (gx - 1, gy))
    gy_dev = ((gx, gy + 1), (gx, gy - 1))

    def place(ref, group, row_off, col_off):
        return ref.at[
            pl.ds(strip * (row_off + 1) + b * (col_off + 1), b), pl.ds(b * group, b)
        ]

    count = [0]

    def remote(src, dst, device):
        number = count[0]
        count[0] += 1
        return pltpu.make_async_remote_copy(
            src_ref=src, dst_ref=dst, send_sem=send_sem.at[number],
            recv_sem=recv_sem.at[number], device_id=device, device_id_type=MESH,
        )

    row_of = (1, 0)
    ou_of = (1, 0)
    ov_of = (1, 0)
    far = (2, 0)
    pairs = ((0, 0, 1, 0), (0, 1, 2, -1), (1, 0, 0, 1), (1, 1, 1, 0))

    gy_early, gy_rhs, gy_late, gx_direct, diag = {}, {}, {}, {}, {}
    for t in (0, 1):
        early, right, late = [], [], []
        ov = far[t]
        early.append(remote(
            masks.at[:, :, pl.ds(ov_of[t], 2)], gy_m.at[t], gy_dev[t]))
        for s in (0, 1):
            early.append(remote(
                rhs.at[row_of[s], far[s], ov], gy_r.at[t, s], gy_dev[t]))
        for s in (0, 1):
            early.append(remote(
                blocks.at[row_of[s], pl.ds(ou_of[s], 2), pl.ds(ov_of[t], 2)],
                gy_c.at[t, row_of[s], pl.ds(ou_of[s], 2)], gy_dev[t]))
        for row, group, ou, row_off in pairs:
            right.append(remote(
                rhs.at[row, ou, ov], place(shadow, group, row_off, 2 * t - 1), gy_dev[t]))
        for s in (0, 1):
            ou = 2 - far[s]
            late.append(remote(
                blocks.at[row_of[s], ou, pl.ds(ov_of[t], 2)],
                gy_c.at[t, row_of[s], ou], gy_dev[t]))
        gy_early[t], gy_rhs[t], gy_late[t] = early, right, late
    for s in (0, 1):
        row_off = 2 * s - 1
        gx_direct[s] = [
            remote(rhs.at[row_of[s], far[s], 1], place(shadow, s, row_off, 0), gx_dev[s]),
            remote(masks.at[row_of[s], pl.ds(ou_of[s], 2)], gx_m.at[s], gx_dev[s]),
            remote(blocks.at[row_of[s], pl.ds(ou_of[s], 2)], gx_c.at[s], gx_dev[s]),
        ]
        for t in (0, 1):
            diag[s, t] = [
                remote(gy_r.at[t, s], place(shadow, s, row_off, 2 * t - 1), gx_dev[s]),
                remote(gy_m.at[t, row_of[s], pl.ds(ou_of[s], 2)], dg_m.at[s, t], gx_dev[s]),
                remote(gy_c.at[t, row_of[s], pl.ds(ou_of[s], 2)], dg_c.at[s, t], gx_dev[s]),
            ]

    barrier = pltpu.get_barrier_semaphore()
    total = jnp.int32(0)
    for exists, device in zip(gx_to + gy_to, gx_dev + gy_dev):
        total = total + exists.astype(jnp.int32)

        @pl.when(exists)
        def _(device=device):
            pl.semaphore_signal(barrier, inc=1, device_id=device, device_id_type=MESH)
    pl.semaphore_wait(barrier, total)

    def start(condition, copies):
        @pl.when(condition)
        def _():
            for copy in copies:
                copy.start()

    for t in (0, 1):
        start(gy_to[t], gy_early[t])
    for s in (0, 1):
        start(gx_to[s], gx_direct[s])

    def sent(condition, copies):
        @pl.when(condition)
        def _():
            for copy in copies:
                copy.wait_send()

    locals_ = [pltpu.make_async_copy(blocks, own_c, local_sem.at[0])]
    for number, (row, group, ou, row_off) in enumerate(pairs):
        locals_.append(pltpu.make_async_copy(
            rhs.at[row, ou, 1], place(shadow, group, row_off, 0), local_sem.at[1 + number]))
    for copy in locals_:
        copy.start()

    def clear(ref):
        ref[...] = jnp.zeros(ref.shape, ref.dtype)

    zero = jnp.zeros((b, b), BF16)
    for group in (0, 1):
        for part in (0, 1):
            for t in (0, 1):
                at = 2 * strip * (1 - group) + b * t
                mid[group, part, 2 * b * t:2 * b * t + b, at:at + 2 * b] = jnp.zeros(
                    (b, 2 * b), BF16)

    def clear_rows(ref):
        def body(index, _):
            ref[pl.ds(index * b, b), :] = jnp.zeros((b, ref.shape[1]), ref.dtype)
            return 0
        lax.fori_loop(0, ref.shape[0] // b, body, 0)

    for ref in (u_second, vec, direc, sol):
        clear_rows(ref)
    clear_rows(v_hi)
    clear_rows(v_lo)
    for ref in (mid, edge):
        for which in (0, 1):
            for part in (0, 1):
                for near in range(ref.shape[-1] // strip):
                    ref[which, part, 0:b, strip * near + 2 * b:strip * near + 3 * b] = zero
                    ref[which, part, 2 * b:3 * b, strip * near:strip * near + b] = zero

    spread = (
        lax.broadcasted_iota(jnp.int32, (atoms, b), 1) // orb
        == lax.broadcasted_iota(jnp.int32, (atoms, b), 0)
    ).astype(F32)

    def widen(value):
        flat = value.astype(F32).reshape(-1, atoms)
        wide = jnp.dot(flat, spread, preferred_element_type=F32)
        return wide.reshape(value.shape[:-1] + (b,))

    def put(w, c, ou, ov, value, mask):
        masked = (value.reshape(b // orb, orb, b) * mask[:, None, :]).reshape(b, b)
        high, low = split(masked)
        base = (0, 0, 1, 2)[w]
        ref, which = ((edge, 0), (mid, 0), (mid, 1), (edge, 1))[w]
        col = strip * (w + ou - 1 - base) + b * (c + ov - 1)
        ref[which, 0, b * c:b * (c + 1), col:col + b] = high
        ref[which, 1, b * c:b * (c + 1), col:col + b] = low

    def finish(condition, copies, otherwise):
        @pl.when(condition)
        def _():
            for copy in copies:
                copy.wait_recv()

        @pl.when(jnp.logical_not(condition))
        def _():
            for ref in otherwise:
                clear(ref)

    locals_[0].wait()
    own_m = widen(own_masks[...])
    for row in (0, 1):
        for ou in range(3):
            for ov in range(3):
                put(row + 1, 1, ou, ov, own_c[row, ou, ov], own_m[row, ou, ov])

    for t in (0, 1):
        sent(gy_to[t], gy_early[t])
        start(gy_to[t], gy_rhs[t])
    for s in (0, 1):
        for t in (0, 1):
            @pl.when(gy_from[t])
            def _(s=s, t=t):
                if s == 0:
                    gy_early[t][0].wait_recv()
                gy_early[t][1 + s].wait_recv()
                gy_early[t][3 + s].wait_recv()
            start(jnp.logical_and(gy_from[t], gx_to[s]), diag[s, t])
    for t in (0, 1):
        sent(gy_to[t], gy_rhs[t])
        start(gy_to[t], gy_late[t])

    for s in (0, 1):
        finish(gx_from[s], gx_direct[s],
               [place(shadow, s, 2 * s - 1, 0), gx_m.at[s], gx_c.at[s]])
        wide = widen(gx_m[s])
        for ou in range(2):
            for ov in range(3):
                put(3 * s, 1, ou + ou_of[s], ov, gx_c[s, ou, ov], wide[ou, ov])

    for t in (0, 1):
        @pl.when(jnp.logical_not(gy_from[t]))
        def _(t=t):
            clear(gy_m.at[t])
            for s in (0, 1):
                for ou in range(2):
                    for ov in range(2):
                        clear(gy_c.at[t, row_of[s], ou + ou_of[s], ov])
        gy_wide = widen(gy_m[t])
        for s in (0, 1):
            for ou in range(2):
                for ov in range(2):
                    at = (t, row_of[s], ou + ou_of[s], ov)
                    put(row_of[s] + 1, 2 * t, at[2], ov + ov_of[t], gy_c[at], gy_wide[at[1:]])
    for t in (0, 1):
        for s in (0, 1):
            finish(jnp.logical_and(gx_from[s], gy_from[t]), diag[s, t],
                   [place(shadow, s, 2 * s - 1, 2 * t - 1), dg_m.at[s, t], dg_c.at[s, t]])
            wide = widen(dg_m[s, t])
            for ou in range(2):
                for ov in range(2):
                    put(3 * s, 2 * t, ou + ou_of[s], ov + ov_of[t],
                        dg_c[s, t, ou, ov], wide[ou, ov])
    for copy in locals_[1:]:
        copy.wait()
    for t in (0, 1):
        finish(gy_from[t], gy_rhs[t],
               [place(shadow, group, row_off, 2 * t - 1) for _, group, _, row_off in pairs])
    def over_chunks(body, sums):
        def step(index, carry):
            return body(pl.ds(pl.multiple_of(index * CHUNK, CHUNK), CHUNK), index * CHUNK, carry)
        return lax.fori_loop(
            0, rows // CHUNK, step, tuple(jnp.zeros((8, 2 * b), F32) for _ in range(sums)))

    def fold(value):
        return jnp.sum(value.reshape(CHUNK // 8, 8, 2 * b), axis=0)

    def column(value):
        return jnp.sum(value, axis=0, keepdims=True)

    def store_split(first, value):
        high, low = split(value)
        for ref, part in ((v_hi, high), (v_lo, low)):
            ref[pl.ds(pl.multiple_of(first, CHUNK), CHUNK), 0:b] = part[:, 0:b]
            ref[pl.ds(pl.multiple_of(first + strip, CHUNK), CHUNK), b:2 * b] = part[:, b:]

    def product(left, right):
        return jnp.dot(left, right, preferred_element_type=F32)

    def apply():
        for w in range(4):
            if w in (0, 3):
                which = w // 3
                near = pl.ds(2 * strip * which, 2 * strip)
                cols = slice(b * which, b * (which + 1))
                high, low = edge[which, 0], edge[which, 1]
            else:
                near = pl.ds(strip * (w - 1), 3 * strip)
                cols = slice(0, 2 * b)
                high, low = mid[w - 1, 0], mid[w - 1, 1]
            v_high, v_low = v_hi[near, cols], v_lo[near, cols]
            value = product(high, v_high) + product(low, v_high) + product(high, v_low)
            if w < 3:
                res[strip * w:strip * (w + 1), 0:b] = value[:, 0:b]
            if w > 0:
                res[strip * (w - 1):strip * w, b:2 * b] = value[:, -b:]

    def prepare(at, first, sums):
        value = shadow[at, :]
        w_vec[at, :] = value
        y_first[at, :] = value
        store_split(first, value)
        return (sums[0] + fold(value * value),)

    norm = column(over_chunks(prepare, 1)[0])
    limit = jnp.concatenate(
        [widen(jnp.broadcast_to(limits[group], (atoms, atoms)))[0:1] for group in (0, 1)], axis=1)
    apply()
    for t in (0, 1):
        finish(gy_from[t], gy_late[t],
               [gy_c.at[t, row_of[s], 2 - far[s]] for s in (0, 1)])
        gy_wide = widen(gy_m[t])
        for s in (0, 1):
            for ov in range(2):
                at = (t, row_of[s], 2 - far[s], ov)
                put(row_of[s] + 1, 2 * t, at[2], ov + ov_of[t], gy_c[at], gy_wide[at[1:]])
    for group in (0, 1):
        for t in (0, 1):
            here = pl.ds(b * 2 * t, b)
            cols = pl.ds(2 * strip * (1 - group) + b * t, 2 * b)
            source = pl.ds(strip * (2 - group) + b * t, 2 * b)
            v_high, v_low = v_hi[source, :], v_lo[source, :]
            high, low = mid[group, 0, here, cols], mid[group, 1, here, cols]
            value = product(high, v_high) + product(low, v_high) + product(high, v_low)
            for k in (0, 1):
                into, lanes = pl.ds(strip * (group + 1 - k) + b * 2 * t, b), pl.ds(b * k, b)
                res[into, lanes] = res[into, lanes] + value[:, b * k:b * (k + 1)]

    def iteration(index, carry):
        rho, beta, tau, theta, eta, ratio = carry
        active = (limit > index.astype(F32)).astype(F32)

        @pl.when(index > 0)
        def _():
            apply()

        def after_first(at, first, sums):
            image = y_first[at, :] - res[at, :]
            u_first[at, :] = image
            value = image + beta * (u_second[at, :] + beta * vec[at, :])
            vec[at, :] = value
            return sums[0] + fold(value * value), sums[1] + fold(shadow[at, :] * value)

        square, along = (column(v) for v in over_chunks(after_first, 2))
        alpha = guarded(rho, along, 0.1 * jnp.sqrt(norm * (square + 1e-06)))
        ratio = guarded(1.0, alpha, 0.1)
        keep = theta * theta * eta * ratio

        def between(at, first, sums):
            y_one = y_first[at, :]
            residual = w_vec[at, :] - alpha * u_first[at, :]
            w_vec[at, :] = residual
            direc[at, :] = y_one + keep * direc[at, :]
            second = y_one - alpha * vec[at, :]
            y_second[at, :] = second
            store_split(first, second)
            return (sums[0] + fold(residual * residual),)

        size = column(over_chunks(between, 1)[0])

        def turn(size, tau):
            theta = jnp.sqrt(size) / tau
            cosine = 1.0 / jnp.sqrt(1.0 + theta * theta)
            return theta, tau * theta * cosine, cosine * cosine * alpha

        theta, tau, eta = turn(size, tau)
        eta_one = active * eta
        apply()

        def after_second(at, first, sums):
            image = y_second[at, :] - res[at, :]
            u_second[at, :] = image
            residual = w_vec[at, :] - alpha * image
            w_vec[at, :] = residual
            return sums[0] + fold(residual * residual), sums[1] + fold(shadow[at, :] * residual)

        size, rho_next = (column(v) for v in over_chunks(after_second, 2))
        keep = theta * theta * eta * ratio
        theta, tau, eta = turn(size, tau)
        eta_two = active * eta
        return keep, eta_one, eta_two, rho_next, size, tau, theta, eta, ratio

    def close(beta, keep, eta_one, eta_two):
        def body(at, first, sums):
            one, second = direc[at, :], y_second[at, :]
            two = second + keep * one
            direc[at, :] = two
            sol[at, :] = sol[at, :] + eta_one * one + eta_two * two
            value = w_vec[at, :] + beta * second
            y_first[at, :] = value
            store_split(first, value)
            return sums
        over_chunks(body, 0)

    zero_row = jnp.zeros_like(norm)

    def whole(index, carry):
        rho, floor, beta, tau, theta, eta, ratio = carry
        keep, eta_one, eta_two, rho_next, size, tau, theta, eta, ratio = iteration(
            index, (rho, beta, tau, theta, eta, ratio))
        beta = guarded(rho_next, rho, floor)
        floor = 0.1 * jnp.sqrt(norm * size)
        close(beta, keep, eta_one, eta_two)
        return rho_next, floor, beta, tau, theta, eta, ratio

    lax.fori_loop(0, ITERS, whole, (
        norm, 0.1 * norm, zero_row, jnp.sqrt(norm), zero_row, zero_row, zero_row))

    def write(index, _):
        at = pl.ds(pl.multiple_of(index * b, b), b)
        out[0, index] = sol[at, 0:b]
        out[1, index] = sol[at, b:2 * b]
        return 0

    lax.fori_loop(0, 9, write, 0)

    for t in (0, 1):
        sent(gy_to[t], gy_late[t])
    for s in (0, 1):
        sent(gx_to[s], gx_direct[s])
        for t in (0, 1):
            sent(jnp.logical_and(gy_from[t], gx_to[s]), diag[s, t])


def shards(blocks, pair_mask, rhs_rows, counts):
    groups = blocks.shape[0]
    b = blocks.shape[-1]
    atoms = pair_mask.shape[-1]
    blocks = blocks.reshape(groups, 3, 3, b, b)
    rhs = rhs_rows.reshape(groups, 3, 3, b, b)
    masks = pair_mask.reshape(groups, 3, 3, atoms, atoms)
    field = pltpu.VMEM((9 * b, 2 * b), F32)
    any_spec = pl.BlockSpec(memory_space=pl.ANY)
    vmem_spec = pl.BlockSpec(memory_space=pltpu.VMEM)
    copies = 2 * 11 + 2 * 3 + 4 * 3
    solved = pl.pallas_call(
        kernel,
        out_shape=pltpu.VMEM((groups, 9, b, b), F32),
        in_specs=[any_spec, any_spec, any_spec, vmem_spec, vmem_spec],
        out_specs=vmem_spec,
        scratch_shapes=[
            pltpu.VMEM((groups, 3, 3, b, b), F32),
            pltpu.VMEM((2, groups, 3, 2, b, b), F32),
            pltpu.VMEM((2, 2, 3, b, b), F32),
            pltpu.VMEM((2, 2, 2, 2, b, b), F32),
            pltpu.VMEM((2, groups, 3, 2, atoms, atoms), jnp.int32),
            pltpu.VMEM((2, 2, 3, atoms, atoms), jnp.int32),
            pltpu.VMEM((2, 2, 2, 2, atoms, atoms), jnp.int32),
            pltpu.VMEM((2, 2, b, b), F32),
            pltpu.VMEM((2, 2, 3 * b, 9 * b), BF16),
            pltpu.VMEM((2, 2, 3 * b, 6 * b), BF16),
            pltpu.VMEM((12 * b, 2 * b), BF16),
            pltpu.VMEM((12 * b, 2 * b), BF16),
            field, field, field, field, field, field, field, field, field, field,
            pltpu.SemaphoreType.DMA((copies,)),
            pltpu.SemaphoreType.DMA((copies,)),
            pltpu.SemaphoreType.DMA((5,)),
        ],
        compiler_params=pltpu.CompilerParams(
            collective_id=0, has_side_effects=True, vmem_limit_bytes=60 * 1024 * 1024
        ),
    )(blocks, masks, rhs, counts, masks)
    return solved.reshape(groups, 1, 9, b, b)


def solution(mesh):
    spec = P("gx", "gy", None, None, None)
    return jax.shard_map(
        shards,
        mesh=mesh,
        in_specs=(spec, spec, spec, P("gx", "gy", None)),
        out_specs=spec,
        check_vma=False,
    )
```

profile of v0, /device:TPU:13, one launch (start us, length us, event | category | flops | bytes accessed | tf_op | source)
XLA Modules:
  0.0 83.2 jit_solution(11194625700142952051)
XLA Ops:
  0.0 1.6 %copy.5 = s32[2,1,9,8,8]{4,3,2,0,1:T(8,128)} copy(s32[2,1,9,8,8]{2,4,3,1,0:T(8,128)} %param.5) | data formatting | bytes 9216 | tf_op args[1]
  1.6 80.5 %shard_map.46 = f32[2,9,128,128]{3,2,1,0:T(8,128)S(1)} custom-call(f32[2,3,3,128,128]{4,3,2,1,0:T(8,128)} %bitcast.7, s32[2,3,3,8,8]{4,3,2,1,0:T(8,128)} %bitcast.9, f32[2,3,3,128,128]{4,3,2,1,0:T(8,128)} %bitcast.8, s32[2,1,8]{2,1,0:T(1,128)} %limits.1, s32[2,3,3,8,8]{4,3,2,1,0:T(8,128)} %bitcast.10), custom_call_target="tpu_custom_call" | custom-call | tf_op jit(solution)/shard_map/pallas_call | solution.py:432
  82.2 1.0 %copy.8 = f32[2,1,9,128,128]{4,3,2,1,0:T(8,128)} copy(f32[2,1,9,128,128]{4,3,2,1,0:T(8,128)S(1)} %bitcast.6) | data formatting | bytes 2359296
where the time goes:
time: 83.7 us; the launch traced here: 83.2 us
  Pallas kernels  80.5 us (96%)
  local copies, waits for them, and re-layouts  2.65 us (3%)
    pallas_call x1, Pallas kernels, shards(): pl.pallas_call(kernel, out_shape=pltpu.VMEM((groups, 9, b, b), F32), in_s...  80.5 us
    unnamed x2, local copies, waits for them, and re-layouts  2.65 us

commit v1 on v0

v1 whole, which is shorter than its diff:
```python
import jax
import jax.numpy as jnp
from jax import lax
from jax.experimental import pallas as pl
from jax.experimental.pallas import tpu as pltpu
from jax.sharding import PartitionSpec as P

ITERS = 3
MESH = pl.DeviceIdType.MESH
F32 = jnp.float32
BF16 = jnp.bfloat16


def guarded(top, bottom, floor_val):
    return top * bottom / (bottom * bottom + floor_val * floor_val)


def split(value):
    high = value.astype(BF16)
    return high, (value - high.astype(F32)).astype(BF16)


def product(left, right):
    return jnp.dot(left, right, preferred_element_type=F32)


ROW_OF = (1, 0)
OU_OF = (1, 0)
EDGE = (2, 0)
PAIRS = ((0, 0, 1, 0), (0, 1, 2, -1), (1, 0, 0, 1), (1, 1, 1, 0))


def sources(s):
    return range(max(0, s - 1), min(3, s + 2))


def kernel(
    blocks, masks, rhs, limits, own_masks, out,
    own_c, g_c, n_c0, n_c1, f_c0, f_c1, d_c, passing,
    o_r, g_r, n_r, f_r, d_r, n_m, f_m, g_m, d_m, own_w,
    shared, single0, single1, single2, single3, vec, basis,
    send_sem, recv_sem, local_sem,
):
    b = blocks.shape[-1]
    atoms = masks.shape[-1]
    orb = b // atoms
    gx, gy = lax.axis_index("gx"), lax.axis_index("gy")
    ngx, ngy = lax.axis_size("gx"), lax.axis_size("gy")
    assert ngy % 2 == 0
    half = ngy // 2
    odd = gy % 2
    sign = 1 - 2 * odd
    gx_to = (gx < ngx - 1, gx > 0)
    gx_from = (gx > 0, gx < ngx - 1)
    gx_dev = ((gx + 1, gy), (gx - 1, gy))
    near_dev, far_dev, hop_dev = (gx, gy + sign), (gx, gy - sign), (gx, gy + 2 * sign)

    def inside(index):
        return jnp.logical_and(index >= 0, index < ngy)

    has_far = inside(gy - sign)
    has_hop = inside(gy + 2 * sign)
    place_in = gy // 2
    rank = jnp.where(odd == 0, place_in, half - 1 - place_in)
    mine_relayed = (4 * rank) // half
    partner_relayed = (4 * (half - 1 - rank)) // half

    def turned(k):
        return 1 if k == 1 else 2 * odd + sign * k

    numbers = {}

    def number(kind, name):
        return numbers.setdefault((kind, name), sum(1 for key in numbers if key[0] == kind))

    def remote(src, dst, device, name, arrival=None):
        return pltpu.make_async_remote_copy(
            src_ref=src, dst_ref=dst, send_sem=send_sem.at[number("send", name)],
            recv_sem=recv_sem.at[number("recv", arrival or name)],
            device_id=device, device_id_type=MESH,
        )

    far_groups = []
    for i in range(4):
        row = i % 2
        source, target = ((rhs, f_r), (blocks, f_c1))[i // 2]
        far_groups.append((source.at[row, :, turned(0)], target.at[row]))
    far_direct = [remote(src, dst, far_dev, ("fd", i), ("fg", i))
                  for i, (src, dst) in enumerate(far_groups)]
    far_pass = [remote(src, passing.at[i], near_dev, ("fp", i))
                for i, (src, _) in enumerate(far_groups)]
    far_hop = [remote(passing.at[i], dst, hop_dev, ("fh", i), ("fg", i))
               for i, (_, dst) in enumerate(far_groups)]
    near_mask = [remote(masks.at[:, :, turned(1 + k)], n_m.at[:, :, k], near_dev, ("nm", k))
                 for k in (0, 1)]
    far_mask = [remote(masks.at[:, :, turned(1 - k)], f_m.at[:, :, k], far_dev, ("fm", k))
                for k in (0, 1)]
    near_c0 = [remote(blocks.at[row, :, 1], n_c0.at[row], near_dev, ("n0", row)) for row in (0, 1)]
    far_c0 = [remote(n_c0.at[row], f_c0.at[row], hop_dev, ("f0", row)) for row in (0, 1)]
    near_rd, near_rn, near_1d, near_1n = [], [], [], []
    for h in (0, 1):
        row, ou, edge = ROW_OF[h], OU_OF[h], EDGE[h]
        two, rest, other = pl.ds(ou, 2), 2 - edge, pl.ds(1 - ou, 2)
        near_rd.append(remote(
            rhs.at[row, edge, turned(2)], n_r.at[row, edge], near_dev, ("rd", h)))
        near_rn.append(remote(
            rhs.at[row, other, turned(2)], n_r.at[row, other], near_dev, ("rn", h)))
        near_1d.append(remote(
            blocks.at[row, two, turned(2)], n_c1.at[row, two], near_dev, ("1d", h)))
        near_1n.append(remote(
            blocks.at[row, rest, turned(2)], n_c1.at[row, rest], near_dev, ("1n", h)))
    gx_direct, diag = [], {}
    for h in (0, 1):
        row, two, edge = ROW_OF[h], pl.ds(OU_OF[h], 2), EDGE[h]
        gx_direct.append([
            remote(masks.at[row, two], g_m.at[h], gx_dev[h], ("gm", h)),
            remote(rhs.at[row, edge, 1], g_r.at[h], gx_dev[h], ("gr", h)),
            remote(blocks.at[row, two], g_c.at[h], gx_dev[h], ("gc", h)),
        ])
        for side, (m, r, c0, c1) in enumerate(((n_m, n_r, n_c0, n_c1), (f_m, f_r, f_c0, f_c1))):
            diag[h, side] = [
                remote(m.at[row, two], d_m.at[h, side], gx_dev[h], ("dm", h, side)),
                remote(r.at[row, edge], d_r.at[h, side], gx_dev[h], ("dr", h, side)),
                remote(c0.at[row, two], d_c.at[h, side, 0], gx_dev[h], ("d0", h, side)),
                remote(c1.at[row, two], d_c.at[h, side, 1], gx_dev[h], ("d1", h, side)),
            ]

    barrier = pltpu.get_barrier_semaphore()
    total = jnp.int32(0)
    peers = [(gx_to[h], gx_dev[h]) for h in (0, 1)]
    peers += [(inside(gy + step), (gx, gy + step)) for step in (-2, -1, 1, 2)]
    for exists, device in peers:
        total = total + exists.astype(jnp.int32)

        @pl.when(exists)
        def _(device=device):
            pl.semaphore_signal(barrier, inc=1, device_id=device, device_id_type=MESH)
    pl.semaphore_wait(barrier, total)

    def start(condition, copies):
        @pl.when(condition)
        def _():
            for copy in copies:
                copy.start()

    def arrived(condition, copies, absent=()):
        @pl.when(condition)
        def _():
            for copy in copies:
                copy.wait_recv()

        if absent:
            @pl.when(jnp.logical_not(condition))
            def _():
                for ref in absent:
                    ref[...] = jnp.zeros(ref.shape, ref.dtype)

    both = jnp.logical_and
    for copy in near_mask:
        copy.start()
    start(has_far, far_mask)
    for i in range(4):
        start(both(has_far, i < mine_relayed), [far_pass[i]])
        start(both(has_far, i >= mine_relayed), [far_direct[i]])
    for copy in near_c0 + near_rd + near_rn + near_1d + near_1n:
        copy.start()
    for h in (0, 1):
        start(gx_to[h], gx_direct[h])

    local_c = pltpu.make_async_copy(blocks, own_c, local_sem.at[0])
    local_r = [pltpu.make_async_copy(rhs.at[row, ou, 1], o_r.at[k], local_sem.at[1 + k])
               for k, (row, _, ou, _) in enumerate(PAIRS)]
    for copy in [local_c] + local_r:
        copy.start()

    spread = (
        lax.broadcasted_iota(jnp.int32, (atoms, b), 1) // orb
        == lax.broadcasted_iota(jnp.int32, (atoms, b), 0)
    ).astype(F32)

    def widen(value):
        flat = value.astype(F32).reshape(-1, atoms)
        wide = jnp.dot(flat, spread, preferred_element_type=F32)
        return wide.reshape(value.shape[:-1] + (b,))

    def put(w, s, ou, ov, value, mask):
        masked = (value.reshape(b // orb, orb, b) * mask[:, None, :]).reshape(b, b)
        from_w, at = w + ou - 1, s + ov - 1 - sources(s)[0]
        first = 0
        if w in (1, 2) and from_w in (1, 2):
            ref, first, col = shared, b * (w - 1), 2 * at + from_w - 1
        elif w == 0:
            ref, col = single0, 2 * at + from_w
        elif w == 3:
            ref, col = single3, 2 * at + from_w - 2
        else:
            ref, col = (single1 if w == 1 else single2), at
        for part, piece in enumerate(split(masked)):
            ref[s, part, first:first + b, b * col:b * col + b] = piece

    def put_rhs(group, u, s, value):
        basis[0, b * (3 * s + u):b * (3 * s + u) + b, b * group:b * group + b] = value
        at = b * (4 * s + u + group)
        for part, piece in enumerate(split(value)):
            vec[0, part, at:at + b, b * group:b * group + b] = piece

    local_c.wait()
    own_w[...] = widen(own_masks[...])
    for row in (0, 1):
        for ou in range(3):
            for ov in range(3):
                put(row + 1, 1, ou, ov, own_c[row, ou, turned(ov)], own_w[row, ou, turned(ov)])
    for k, (row, group, ou, off) in enumerate(PAIRS):
        local_r[k].wait()
        put_rhs(group, off + 1, 1, o_r[k])

    for h in (0, 1):
        arrived(gx_from[h], gx_direct[h], [g_m.at[h], g_r.at[h], g_c.at[h]])
        own_w[h, 0:2] = widen(g_m[h])
        for ou in range(2):
            for ov in range(3):
                put(3 * h, 1, ou + OU_OF[h], ov, g_c[h, ou, turned(ov)], own_w[h, ou, turned(ov)])
        put_rhs(h, 2 * h, 1, g_r[h])

    for k in (0, 1):
        near_mask[k].wait_recv()
    for h in (0, 1):
        start(gx_to[h], diag[h, 0][0:1])
    for i in range(4):
        @pl.when(i < partner_relayed)
        def _(i=i):
            far_pass[i].wait_recv()
            far_hop[i].start()
    n_wide = widen(n_m[...])
    for h in (1, 0):
        row = ROW_OF[h]
        near_c0[row].wait_recv()
        start(has_hop, [far_c0[row]])
        start(gx_to[h], diag[h, 0][2:3])
        for ou in range(3):
            put(row + 1, 2, ou, 1, n_c0[row, ou], n_wide[row, ou, 0])
    arrived(has_far, far_mask, [f_m])
    for h in (0, 1):
        start(both(has_far, gx_to[h]), diag[h, 1][0:1])
    f_wide = widen(f_m[...])
    for row in (0, 1):
        arrived(has_far, [far_direct[row]], [f_r.at[row]])
        h = 1 - row
        start(both(has_far, gx_to[h]), diag[h, 1][1:2])
    for h in (0, 1):
        near_rd[h].wait_recv()
        start(gx_to[h], diag[h, 0][1:2])
    for row in (0, 1):
        arrived(has_far, [far_direct[2 + row]], [f_c1.at[row]])
        h = 1 - row
        start(both(has_far, gx_to[h]), diag[h, 1][3:4])
        for ou in range(3):
            put(row + 1, 0, ou, 2, f_c1[row, ou], f_wide[row, ou, 1])
    for row in (0, 1):
        arrived(has_far, [far_c0[row]], [f_c0.at[row]])
        h = 1 - row
        start(both(has_far, gx_to[h]), diag[h, 1][2:3])
        for ou in range(3):
            put(row + 1, 0, ou, 1, f_c0[row, ou], f_wide[row, ou, 0])
    for h in (0, 1):
        near_rn[h].wait_recv()
    for row, group, ou, off in PAIRS:
        put_rhs(group, off + 1, 2, n_r[row, ou])
        put_rhs(group, off + 1, 0, f_r[row, ou])
    for h in (0, 1):
        near_1d[h].wait_recv()
        start(gx_to[h], diag[h, 0][3:4])
    for h in (0, 1):
        row = ROW_OF[h]
        for ou in (OU_OF[h], OU_OF[h] + 1):
            put(row + 1, 2, ou, 0, n_c1[row, ou], n_wide[row, ou, 1])

    def corner(h, side):
        arrived(gx_from[h] if side == 0 else both(gx_from[h], has_far), diag[h, side],
                [d_m.at[h, side], d_r.at[h, side], d_c.at[h, side]])
        wide = widen(d_m[h, side])
        s = 2 - 2 * side
        for k in (0, 1):
            for ou in range(2):
                put(3 * h, s, ou + OU_OF[h], 1 if k == 0 else 2 * side,
                    d_c[h, side, k, ou], wide[ou, k])
        put_rhs(h, 2 * h, s, d_r[h, side])

    for side in (1, 0):
        for h in (0, 1):
            corner(h, side)
    for h in (0, 1):
        near_1n[h].wait_recv()
        row, ou = ROW_OF[h], 2 - EDGE[h]
        put(row + 1, 2, ou, 0, n_c1[row, ou], n_wide[row, ou, 1])

    def fold(value):
        return jnp.sum(value.reshape(-1, 8, 2 * b), axis=0)

    def column(value):
        return jnp.sum(value, axis=0, keepdims=True)

    def at_of(s, u):
        return pl.ds(b * (3 * s + u), b)

    def apply_rows(turn, s):
        count = len(sources(s))

        def tall(part, w, strips, lanes):
            return jnp.concatenate(
                [vec[turn, part, b * (4 * k + w):b * (4 * k + w + strips), lanes] for k in sources(s)],
                axis=0)

        every = slice(0, 2 * b)
        high, low = tall(0, 1, 2, every), tall(1, 1, 2, every)
        c_high = shared[s, 0, :, 0:2 * b * count]
        c_low = shared[s, 1, :, 0:2 * b * count]
        joint = product(
            jnp.concatenate([c_high, c_low, c_high], axis=1),
            jnp.concatenate([high, high, low], axis=0))

        def alone(ref, w, strips, group):
            lanes = slice(b * group, b * group + b)
            right = jnp.concatenate([tall(0, w, strips, lanes), tall(1, w, strips, lanes)], axis=1)
            width = b * strips * count
            left = jnp.concatenate([ref[s, 0, :, 0:width], ref[s, 1, :, 0:width]], axis=1)
            value = product(left, jnp.concatenate([right, right], axis=0))
            return value[:, 0:b] + value[:, b:2 * b]

        first, second = joint[0:b], joint[b:2 * b]
        return (
            jnp.concatenate([alone(single0, 0, 2, 0), first[:, b:]], axis=1),
            jnp.concatenate([first[:, 0:b] + alone(single1, 0, 1, 0),
                             second[:, b:] + alone(single2, 3, 1, 1)], axis=1),
            jnp.concatenate([second[:, 0:b], alone(single3, 2, 2, 1)], axis=1),
        )

    gram = {}

    def power(j):
        sums = [jnp.zeros((8, 2 * b), F32) for _ in range(j + 1)]
        for s in (1, 0, 2):
            for u, value in enumerate(apply_rows((j - 1) % 2, s)):
                basis[j, at_of(s, u), :] = value
                for part, piece in enumerate(split(value)):
                    for group in (0, 1):
                        at = b * (4 * s + u + group)
                        vec[j % 2, part, at:at + b, b * group:b * group + b] = (
                            piece[:, b * group:b * group + b])
                for i in range(j):
                    sums[i] = sums[i] + fold(value * basis[i, at_of(s, u), :])
                sums[j] = sums[j] + fold(value * value)
        for i in range(j + 1):
            gram[i, j] = gram[j, i] = column(sums[i])

    def add(left, factor, right):
        size = max(len(left), len(right))
        result = []
        for k in range(size):
            a = left[k] if k < len(left) else None
            c = right[k] if k < len(right) else None
            if c is None:
                result.append(a)
            else:
                result.append(factor * c if a is None else a + factor * c)
        return result

    def image(value):
        return add(list(value) + [None], -1.0, [None] + list(value))

    def inner(left, other):
        result = None
        for i, a in enumerate(left):
            for k, c in enumerate(other):
                if a is None or c is None:
                    continue
                term = (a * c) * gram[i, k]
                result = term if result is None else result + term
        return result

    def norm_of(value):
        result = None
        for i, a in enumerate(value):
            for k in range(i, len(value)):
                term = (a * value[k]) * gram[i, k] * (1.0 if i == k else 2.0)
                result = term if result is None else result + term
        return jnp.maximum(result, 0.0)

    start_sums = jnp.zeros((8, 2 * b), F32)
    for s in range(3):
        for u in range(3):
            value = basis[0, at_of(s, u), :]
            start_sums = start_sums + fold(value * value)
    gram[0, 0] = column(start_sums)
    limit = jnp.concatenate(
        [widen(jnp.broadcast_to(limits[group], (atoms, atoms)))[0:1] for group in (0, 1)], axis=1)

    power(1)
    norm = gram[0, 0]
    one = jnp.ones_like(norm)
    shadow = [one]
    resid = [one]
    y_first = [one]
    rho, floor = norm, 0.1 * norm
    tau = jnp.sqrt(norm)
    theta = eta = jnp.zeros_like(norm)
    u_first = image(y_first)
    along = u_first
    direc, sol = [], []
    y_second = u_second = None
    for n in range(1, ITERS + 1):
        active = (limit >= float(n)).astype(F32)
        if n > 1:
            power(2 * n - 1)
            rho_next = inner(shadow, resid)
            beta = guarded(rho_next, rho, floor)
            floor = 0.1 * jnp.sqrt(norm * size)
            rho = rho_next
            y_first = add(resid, beta, y_second)
            u_first = image(y_first)
            along = add(u_first, beta, add(u_second, beta, along))
        alpha = guarded(rho, inner(shadow, along), 0.1 * jnp.sqrt(norm * (norm_of(along) + 1e-06)))
        ratio = guarded(1.0, alpha, 0.1)
        y_second = add(y_first, -alpha, along)
        u_second = image(y_second)
        for part, (y, u) in enumerate(((y_first, u_first), (y_second, u_second))):
            resid = add(resid, -alpha, u)
            direc = add(y, theta * theta * eta * ratio, direc)
            if part == 1 and n < ITERS:
                power(2 * n)
            if part == 1 and n == ITERS:
                sums = jnp.zeros((8, 2 * b), F32)
                for s in (1, 0, 2):
                    for r, value in enumerate(apply_rows((2 * n - 1) % 2, s)):
                        value = value * resid[2 * n]
                        for i in range(2 * n):
                            value = value + basis[i, at_of(s, r), :] * resid[i]
                        sums = sums + fold(value * value)
                size = column(sums)
            else:
                size = norm_of(resid)
            theta = jnp.sqrt(size) / tau
            cosine = 1.0 / jnp.sqrt(1.0 + theta * theta)
            tau = tau * theta * cosine
            eta = cosine * cosine * alpha
            sol = add(sol, active * eta, direc)

    for s in range(3):
        for u in range(3):
            value = basis[0, at_of(s, u), :] * sol[0]
            for i in range(1, 2 * ITERS):
                value = value + basis[i, at_of(s, u), :] * sol[i]
            for group in (0, 1):
                out[group, 3 * u + turned(s)] = value[:, b * group:b * group + b]

    for copy in near_mask + near_c0 + near_rd + near_rn + near_1d + near_1n:
        copy.wait_send()

    def sent(condition, copies):
        @pl.when(condition)
        def _():
            for copy in copies:
                copy.wait_send()

    sent(has_far, far_mask)
    sent(has_hop, far_c0)
    for i in range(4):
        sent(both(has_far, i < mine_relayed), [far_pass[i]])
        sent(both(has_far, i >= mine_relayed), [far_direct[i]])
        sent(i < partner_relayed, [far_hop[i]])
    for h in (0, 1):
        sent(gx_to[h], gx_direct[h] + diag[h, 0])
        sent(both(gx_to[h], has_far), diag[h, 1])
    assert len(numbers) <= 2 * COPIES


COPIES = 56


def shards(blocks, pair_mask, rhs_rows, counts):
    groups = blocks.shape[0]
    b = blocks.shape[-1]
    atoms = pair_mask.shape[-1]
    blocks = blocks.reshape(groups, 3, 3, b, b)
    rhs = rhs_rows.reshape(groups, 3, 3, b, b)
    masks = pair_mask.reshape(groups, 3, 3, atoms, atoms)
    any_spec = pl.BlockSpec(memory_space=pl.ANY)
    vmem_spec = pl.BlockSpec(memory_space=pltpu.VMEM)

    def raw(*lead):
        return pltpu.VMEM(lead + (b, b), F32)

    def flags(*lead):
        return pltpu.VMEM(lead + (atoms, atoms), jnp.int32)

    solved = pl.pallas_call(
        kernel,
        out_shape=pltpu.VMEM((groups, 9, b, b), F32),
        in_specs=[any_spec, any_spec, any_spec, vmem_spec, vmem_spec],
        out_specs=vmem_spec,
        scratch_shapes=[
            raw(groups, 3, 3), raw(2, 2, 3), raw(groups, 3), raw(groups, 3), raw(groups, 3),
            raw(groups, 3), raw(2, 2, 2, 2), raw(4, 3),
            raw(4), raw(2), raw(groups, 3), raw(groups, 3), raw(2, 2),
            flags(groups, 3, 2), flags(groups, 3, 2), flags(2, 2, 3), flags(2, 2, 2, 2),
            pltpu.VMEM((groups, 3, 3, atoms, b), F32),
            pltpu.VMEM((3, 2, 2 * b, 6 * b), BF16),
            pltpu.VMEM((3, 2, b, 6 * b), BF16),
            pltpu.VMEM((3, 2, b, 3 * b), BF16),
            pltpu.VMEM((3, 2, b, 3 * b), BF16),
            pltpu.VMEM((3, 2, b, 6 * b), BF16),
            pltpu.VMEM((2, 2, 12 * b, 2 * b), BF16),
            pltpu.VMEM((2 * ITERS, 9 * b, 2 * b), F32),
            pltpu.SemaphoreType.DMA((COPIES,)),
            pltpu.SemaphoreType.DMA((COPIES,)),
            pltpu.SemaphoreType.DMA((5,)),
        ],
        compiler_params=pltpu.CompilerParams(
            collective_id=0, has_side_effects=True, vmem_limit_bytes=60 * 1024 * 1024
        ),
    )(blocks, masks, rhs, counts, masks)
    return solved.reshape(groups, 1, 9, b, b)


def solution(mesh):
    spec = P("gx", "gy", None, None, None)
    return jax.shard_map(
        shards,
        mesh=mesh,
        in_specs=(spec, spec, spec, P("gx", "gy", None)),
        out_specs=spec,
        check_vma=False,
    )
```

time: 83.7 us -> 62.2 us (0.74)
  Pallas kernels: 80.5 us -> 58.5 us
    pallas_call x1, Pallas kernels: 80.5 us -> 58.5 us  [shards(): pl.pallas_call(kernel, out_shape=pltpu.VMEM((groups, 9, b, b), F32), in_s...]
where the time goes in v1:
time: 62.2 us; the launch traced here: 61.2 us
  Pallas kernels  58.5 us (94%)
  local copies, waits for them, and re-layouts  2.65 us (4%)
    pallas_call x1, Pallas kernels, shards(): pl.pallas_call(kernel, out_shape=pltpu.VMEM((groups, 9, b, b), F32), in_s...  58.5 us
    unnamed x2, local copies, waits for them, and re-layouts  2.65 us

profile of v1, /device:TPU:13, one launch (start us, length us, event | category | flops | bytes accessed | tf_op | source)
XLA Modules:
  0.0 61.2 jit_solution(17838019138948159581)
XLA Ops:
  0.0 1.6 %copy.5 = s32[2,1,9,8,8]{4,3,2,0,1:T(8,128)} copy(s32[2,1,9,8,8]{2,4,3,1,0:T(8,128)} %param.5) | data formatting | bytes 9216 | tf_op args[1]
  1.6 58.5 %shard_map.46 = f32[2,9,128,128]{3,2,1,0:T(8,128)S(1)} custom-call(f32[2,3,3,128,128]{4,3,2,1,0:T(8,128)} %bitcast.7, s32[2,3,3,8,8]{4,3,2,1,0:T(8,128)} %bitcast.9, f32[2,3,3,128,128]{4,3,2,1,0:T(8,128)} %bitcast.8, s32[2,1,8]{2,1,0:T(1,128)} %limits.1, s32[2,3,3,8,8]{4,3,2,1,0:T(8,128)} %bitcast.10), custom_call_target="tpu_custom_call" | custom-call | tf_op jit(solution)/shard_map/pallas_call | solution.py:496
  60.2 1.0 %copy.8 = f32[2,1,9,128,128]{4,3,2,1,0:T(8,128)} copy(f32[2,1,9,128,128]{4,3,2,1,0:T(8,128)S(1)} %bitcast.6) | data formatting | bytes 2359296

commit v2 on v0

v2 whole, which is shorter than its diff:
```python
import jax
import jax.numpy as jnp
from jax import lax
from jax.experimental import pallas as pl
from jax.experimental.pallas import tpu as pltpu
from jax.sharding import PartitionSpec as P

ITERS = 3
COPIES = 80
MESH = pl.DeviceIdType.MESH
F32 = jnp.float32
BF16 = jnp.bfloat16


def guarded(top, bottom, floor_val):
    return top * bottom / (bottom * bottom + floor_val * floor_val)


def split(value):
    high = value.astype(BF16)
    return high, (value - high.astype(F32)).astype(BF16)


def product(left, right):
    return jnp.dot(left, right, preferred_element_type=F32)


def near_three(s):
    return range(max(0, s - 1), min(3, s + 2))


def add(left, factor, right):
    result = []
    for k in range(max(len(left), len(right))):
        a = left[k] if k < len(left) else None
        c = right[k] if k < len(right) else None
        if c is None:
            result.append(a)
        else:
            result.append(factor * c if a is None else a + factor * c)
    return result


def image(value):
    return add(list(value) + [None], -1.0, [None] + list(value))


def kernel(
    blocks, masks, rhs, limits, own_masks, out,
    own_c, g_c, n_c0, n_c1, f_c0, f_c1, d_c, passing,
    o_r, g_r, n_r, f_r, d_r, n_m, f_m, g_m, d_m, wide,
    c_of0, c_of1, c_of2, c_of3, vec, basis,
    send_sem, recv_sem, local_sem,
):
    b = blocks.shape[-1]
    atoms = masks.shape[1]
    offsets = masks.shape[-1]
    orb = b // atoms
    gx, gy = lax.axis_index("gx"), lax.axis_index("gy")
    ngx, ngy = lax.axis_size("gx"), lax.axis_size("gy")
    assert ngx % 2 == 0 and ngy % 2 == 0
    half = ngy // 2
    core, odd = gx % 2, gy % 2
    step_x, step_y = 1 - 2 * core, 1 - 2 * odd
    inner_dev, outer_dev = (gx + step_x, gy), (gx - step_x, gy)
    near_dev, far_dev, hop_dev = (gx, gy + step_y), (gx, gy - step_y), (gx, gy + 2 * step_y)

    def inside(index, size):
        return jnp.logical_and(index >= 0, index < size)

    both = jnp.logical_and
    has_outer = inside(gx - step_x, ngx)
    has_far = inside(gy - step_y, ngy)
    has_hop = inside(gy + 2 * step_y, ngy)
    side_there = (None, has_far)
    rank = jnp.where(odd == 0, gy // 2, half - 1 - gy // 2)
    mine_relayed = (4 * rank) // half
    partner_relayed = (4 * (half - 1 - rank)) // half

    def ty(j):
        return 1 if j == 1 else 2 * odd + step_y * j

    def tx(k):
        return 1 if k == 1 else 2 * (1 - core) - step_x * k

    rows = (1 - core, core)
    head, tail = pl.ds(1 - core, 2), pl.ds(core, 2)
    full = pl.ds(0, 3)

    numbers = {}

    def number(kind, name):
        return numbers.setdefault((kind, name), sum(1 for key in numbers if key[0] == kind))

    def remote(src, dst, device, name, arrival=None):
        return pltpu.make_async_remote_copy(
            src_ref=src, dst_ref=dst, send_sem=send_sem.at[number("send", name)],
            recv_sem=recv_sem.at[number("recv", arrival or name)],
            device_id=device, device_id_type=MESH,
        )

    n_mask = remote(masks, n_m, near_dev, "nm")
    f_mask = remote(n_m, f_m, hop_dev, "fm")
    far_parts = (
        (0, rhs, f_r, rows[0], head, (0, 2)), (0, rhs, f_r, rows[1], pl.ds(tx(0), 1), (2, 1)),
        (1, blocks, f_c1, rows[0], full, (3, 3)),
        (2, rhs, f_r, rows[1], tail, (6, 2)), (2, rhs, f_r, rows[0], pl.ds(tx(2), 1), (8, 1)),
        (4, blocks, f_c1, rows[1], head, None), (4, blocks, f_c1, rows[1], pl.ds(tx(2), 1), None),
    )
    far_direct, far_pass, far_hop, far_group = [], [], [], []
    for i, (group, source, target, row, ous, slot) in enumerate(far_parts):
        src, dst = source.at[row, ous, ty(0)], target.at[row, ous]
        far_group.append(group)
        far_direct.append(remote(src, dst, far_dev, ("fd", i), ("fg", i)))
        if slot is not None:
            held = passing.at[pl.ds(*slot)]
            far_pass.append(remote(src, held, near_dev, ("fp", i)))
            far_hop.append(remote(held, dst, hop_dev, ("fh", i), ("fg", i)))

    c_parts = ((rows[0], full), (rows[1], head), (rows[1], pl.ds(tx(2), 1)))
    near_c0 = [remote(blocks.at[row, ous, 1], n_c0.at[row, ous], near_dev, ("n0", i))
               for i, (row, ous) in enumerate(c_parts)]
    near_c1 = [remote(blocks.at[row, ous, ty(2)], n_c1.at[row, ous], near_dev, ("n1", i))
               for i, (row, ous) in enumerate(c_parts)]
    far_c0 = [remote(n_c0.at[row, ous], f_c0.at[row, ous], hop_dev, ("f0", i))
              for i, (row, ous) in enumerate(c_parts)]
    near_r = [remote(rhs.at[row, ous, ty(2)], n_r.at[row, ous], near_dev, ("nr", i))
              for i, (row, ous) in enumerate((
                  (rows[0], head), (rows[1], pl.ds(tx(0), 1)),
                  (rows[1], tail), (rows[0], pl.ds(tx(2), 1))))]

    direct_in = [
        remote(masks.at[rows[0]], g_m.at[0], inner_dev, "gm0"),
        remote(rhs.at[rows[0], tx(0), 1], g_r.at[0], inner_dev, "gr0"),
        remote(blocks.at[rows[0], head], g_c.at[0], inner_dev, "gc0"),
    ]
    direct_out = [
        remote(masks.at[rows[1]], g_m.at[1], outer_dev, "gm1"),
        remote(rhs.at[rows[1], tx(2), 1], g_r.at[1], outer_dev, "gr1"),
        remote(blocks.at[rows[1], tail], g_c.at[1], outer_dev, "gc1"),
    ]
    in_m, in_r, in_c, out_m, out_r, out_mid, out_end = [], [], [], [], [], [], []
    for side, (m, r, coupled) in enumerate(((n_m, n_r, (n_c0, n_c1)), (f_m, f_r, (f_c0, f_c1)))):
        in_m.append(remote(m.at[rows[0]], d_m.at[0, side], inner_dev, ("im", side)))
        in_r.append(remote(r.at[rows[0], tx(0)], d_r.at[0, side], inner_dev, ("ir", side)))
        out_m.append(remote(m.at[rows[1]], d_m.at[1, side], outer_dev, ("om", side)))
        out_r.append(remote(r.at[rows[1], tx(2)], d_r.at[1, side], outer_dev, ("or", side)))
        in_c.append([remote(c.at[rows[0], head], d_c.at[0, side, k], inner_dev, ("ic", side, k))
                     for k, c in enumerate(coupled)])
        out_mid.append([remote(c.at[rows[1], 1], d_c.at[1, side, k, 1 - core], outer_dev, ("oc", side, k))
                        for k, c in enumerate(coupled)])
        out_end.append([remote(c.at[rows[1], tx(2)], d_c.at[1, side, k, core], outer_dev, ("oe", side, k))
                        for k, c in enumerate(coupled)])

    barrier = pltpu.get_barrier_semaphore()
    total = jnp.int32(0)
    peers = [(inside(gx + step, ngx), (gx + step, gy)) for step in (-1, 1)]
    peers += [(inside(gy + step, ngy), (gx, gy + step)) for step in (-2, -1, 1, 2)]
    for exists, device in peers:
        total = total + exists.astype(jnp.int32)

        @pl.when(exists)
        def _(device=device):
            pl.semaphore_signal(barrier, inc=1, device_id=device, device_id_type=MESH)
    pl.semaphore_wait(barrier, total)

    def on(condition, actions):
        if condition is None:
            for action in actions:
                action()
        else:
            @pl.when(condition)
            def _():
                for action in actions:
                    action()

    def start(condition, *copies):
        on(condition, [copy.start for copy in copies])

    def arrived(condition, *copies):
        on(condition, [copy.wait_recv for copy in copies])

    def sent(condition, *copies):
        on(condition, [copy.wait_send for copy in copies])

    def is_relayed(i):
        return far_group[i] < mine_relayed

    def start_pass(group):
        for i, copy in enumerate(far_pass):
            if far_group[i] == group:
                start(is_relayed(i), copy)

    def start_direct(i):
        start(both(has_far, jnp.logical_not(is_relayed(i))), far_direct[i])

    def relay(group):
        for i, copy in enumerate(far_pass):
            if far_group[i] == group:
                @pl.when(group < partner_relayed)
                def _(i=i, copy=copy):
                    copy.wait_recv()
                    far_hop[i].start()

    n_mask.start()
    start_pass(0)
    start(None, near_c0[0], near_c0[1])
    start_pass(1)
    start(None, near_r[0], near_r[1], near_c1[0], near_c1[1])
    for i in (0, 1, 2, 5):
        start_direct(i)
    start(None, *direct_in)
    start(has_outer, *direct_out)
    start_pass(2)
    start(None, near_c0[2], near_c1[2], near_r[2], near_r[3])
    for i in (6, 3, 4):
        start_direct(i)

    local_c = pltpu.make_async_copy(blocks, own_c, local_sem.at[0])
    own_rhs = ((0, 1, 0, 1), (0, 2, 1, 0), (1, 0, 0, 2), (1, 1, 1, 1))
    local_r = [pltpu.make_async_copy(rhs.at[rows[t], tx(k), 1], o_r.at[i], local_sem.at[1 + i])
               for i, (_, _, t, k) in enumerate(own_rhs)]
    start(None, local_c, *local_r)

    def clear(*refs):
        for ref in refs:
            ref[...] = jnp.zeros(ref.shape, ref.dtype)

    @pl.when(jnp.logical_not(has_far))
    def _():
        clear(f_c0, f_c1, f_r, f_m, *[d.at[x, 1] for d in (d_c, d_r, d_m) for x in (0, 1)])

    @pl.when(jnp.logical_not(has_outer))
    def _():
        clear(g_c.at[1], g_r.at[1], g_m.at[1], d_c.at[1], d_r.at[1], d_m.at[1])

    wide_shape = (atoms * atoms, atoms * b)
    above, across = (lax.broadcasted_iota(jnp.int32, wide_shape, d) for d in (0, 1))
    spread = (above == atoms * (across // b) + across % b // orb).astype(F32)

    def widen(index, value):
        flat = value.astype(F32).reshape(atoms * atoms, offsets)
        wide[index] = lax.dot_general(
            flat, spread, (((0,), (0,)), ((), ())), preferred_element_type=F32)

    c_refs = (c_of0, c_of1, c_of2, c_of3)
    first_row = (0, 0, 1, 2)

    def put(w, s, k, j, value, mask):
        mask_row = wide[mask, pl.ds(3 * tx(k) + ty(j), 1), :]
        found = near_three(s)
        col = b * ((w + k - 1 - first_row[w]) * len(found) + s + j - 1 - found[0])
        for i in range(atoms):
            masked = value[orb * i:orb * (i + 1)] * mask_row[:, b * i:b * (i + 1)]
            for part, piece in enumerate(split(masked)):
                at = b * part + orb * i
                c_refs[w][s, at:at + orb, col:col + b] = piece

    def put_rhs(solve, u, s, value):
        at = b * (3 * u + s)
        basis[solve, 0, at:at + b, :] = value
        for part, piece in enumerate(split(value)):
            vec[solve, 0, at:at + b, b * part:b * part + b] = piece

    local_c.wait()
    for row in (0, 1):
        widen(row, own_masks[row])
    for t in (0, 1):
        for k in range(3):
            for j in range(3):
                put(1 + t, 1, k, j, own_c[rows[t], tx(k), ty(j)], rows[t])
    for i, (solve, u, _, _) in enumerate(own_rhs):
        local_r[i].wait()
        put_rhs(solve, u, 1, o_r[i])

    arrived(None, *direct_in)
    widen(2, g_m[0])
    for k, slot in ((1, 1 - core), (2, core)):
        for j in range(3):
            put(0, 1, k, j, g_c[0, slot, ty(j)], 2)
    put_rhs(0, 0, 1, g_r[0])

    n_mask.wait_recv()
    start(has_hop, f_mask)
    start(None, in_m[0])
    start(has_outer, out_m[0])
    relay(0)
    for row in (0, 1):
        widen(4 + row, n_m[row])

    def put_column(s, ref, t, k, j):
        put(1 + t, s, k, j, ref[rows[t], tx(k)], (4 if s == 2 else 6) + rows[t])

    near_c0[0].wait_recv()
    start(has_hop, far_c0[0])
    start(None, in_c[0][0])
    for k in range(3):
        put_column(2, n_c0, 0, k, 1)
    near_c0[1].wait_recv()
    start(has_hop, far_c0[1])
    start(has_outer, out_mid[0][0])
    for k in (0, 1):
        put_column(2, n_c0, 1, k, 1)
    relay(1)
    arrived(None, near_r[0], near_r[1])
    start(None, in_r[0])
    put_rhs(0, 1, 2, n_r[rows[0], 1])
    put_rhs(0, 2, 2, n_r[rows[1], tx(0)])

    arrived(has_far, f_mask)
    start(has_far, in_m[1])
    start(both(has_far, has_outer), out_m[1])
    for row in (0, 1):
        widen(6 + row, f_m[row])
    arrived(has_far, far_direct[0], far_direct[1])
    start(has_far, in_r[1])
    put_rhs(0, 1, 0, f_r[rows[0], 1])
    put_rhs(0, 2, 0, f_r[rows[1], tx(0)])
    arrived(has_far, far_direct[2])
    start(has_far, in_c[1][1])
    arrived(has_far, far_direct[5])
    start(both(has_far, has_outer), out_mid[1][1])
    for t, ks in ((0, (0, 1, 2)), (1, (0, 1))):
        for k in ks:
            put_column(0, f_c1, t, k, 2)
    arrived(has_far, far_c0[0], far_c0[1])
    start(has_far, in_c[1][0])
    start(both(has_far, has_outer), out_mid[1][0])
    for t, ks in ((0, (0, 1, 2)), (1, (0, 1))):
        for k in ks:
            put_column(0, f_c0, t, k, 1)

    arrived(has_outer, *direct_out)
    widen(3, g_m[1])
    for k, slot in ((1, core), (0, 1 - core)):
        for j in range(3):
            put(3, 1, k, j, g_c[1, slot, ty(j)], 3)
    put_rhs(1, 2, 1, g_r[1])

    near_c1[0].wait_recv()
    start(None, in_c[0][1])
    near_c1[1].wait_recv()
    start(has_outer, out_mid[0][1])
    for t, ks in ((0, (0, 1, 2)), (1, (0, 1))):
        for k in ks:
            put_column(2, n_c1, t, k, 0)

    def put_corner(x, side, ways):
        s = 2 - 2 * side
        for way in ways:
            for k, slot in (((1, 1 - core), (2, core)), ((1, core), (0, 1 - core)))[x]:
                put(3 * x, s, k, 1 if way == 0 else 2 * side, d_c[x, side, way, slot],
                    8 + 2 * x + side)

    for side in (1, 0):
        arrived(side_there[side], in_m[side], in_r[side], *in_c[side])
        widen(8 + side, d_m[0, side])
        put_corner(0, side, (0, 1))
        put_rhs(0, 0, 2 - 2 * side, d_r[0, side])

    def fold(value):
        return jnp.sum(value.reshape(-1, 8, b), axis=0)

    def column(value):
        return jnp.sum(value, axis=0, keepdims=True)

    def at_of(u, s):
        return slice(b * (3 * u + s), b * (3 * u + s) + b)

    members = [(u, s) for s in (1, 0, 2) for u in range(3)]

    def apply_row(solve, turn, u, s):
        found = near_three(s)
        strips = near_three(u)
        left = b * len(found) * (strips[0] + solve - first_row[u + solve])
        width = b * len(found) * len(strips)
        right = [vec[solve, turn, b * (3 * k + found[0]):b * (3 * k + found[0] + len(found)), :]
                 for k in strips]
        value = product(c_refs[u + solve][s, :, left:left + width], jnp.concatenate(right, axis=0))
        return value[0:b, 0:b] + (value[0:b, b:2 * b] + value[b:2 * b, 0:b])

    def solve_cluster(solve, between):
        gram = {}

        def power(j):
            sums = [jnp.zeros((8, b), F32) for _ in range(j + 1)]
            for u, s in members:
                value = apply_row(solve, (j - 1) % 2, u, s)
                basis[solve, j, at_of(u, s), :] = value
                for part, piece in enumerate(split(value)):
                    vec[solve, j % 2, at_of(u, s), b * part:b * part + b] = piece
                for i in range(j):
                    sums[i] = sums[i] + fold(value * basis[solve, i, at_of(u, s), :])
                sums[j] = sums[j] + fold(value * value)
            for i in range(j + 1):
                gram[i, j] = gram[j, i] = column(sums[i])
            between(j)

        def inner(left, other):
            result = None
            for i, a in enumerate(left):
                for k, c in enumerate(other):
                    term = (a * c) * gram[i, k]
                    result = term if result is None else result + term
            return result

        def norm_of(value):
            result = None
            for i, a in enumerate(value):
                for k in range(i, len(value)):
                    term = (a * value[k]) * gram[i, k] * (1.0 if i == k else 2.0)
                    result = term if result is None else result + term
            return jnp.maximum(result, 0.0)

        first_sums = jnp.zeros((8, b), F32)
        for u, s in members:
            value = basis[solve, 0, at_of(u, s), :]
            first_sums = first_sums + fold(value * value)
        gram[0, 0] = column(first_sums)
        counts = limits[rows[solve]].astype(F32)
        atom_of = (lax.broadcasted_iota(jnp.int32, (atoms, b), 1) // orb
                   == lax.broadcasted_iota(jnp.int32, (atoms, b), 0)).astype(F32)
        limit = product(jnp.broadcast_to(counts, (atoms, atoms)), atom_of)[0:1]

        power(1)
        norm = gram[0, 0]
        shadow = [jnp.ones_like(norm)]
        resid = y_first = shadow
        rho, floor = norm, 0.1 * norm
        tau = jnp.sqrt(norm)
        theta = eta = jnp.zeros_like(norm)
        u_first = along = image(y_first)
        direc, sol = [], []
        for n in range(1, ITERS + 1):
            active = (limit >= float(n)).astype(F32)
            if n > 1:
                power(2 * n - 1)
                rho_next = inner(shadow, resid)
                beta = guarded(rho_next, rho, floor)
                floor = 0.1 * jnp.sqrt(norm * size)
                rho = rho_next
                y_first = add(resid, beta, y_second)
                u_first = image(y_first)
                along = add(u_first, beta, add(u_second, beta, along))
            alpha = guarded(
                rho, inner(shadow, along), 0.1 * jnp.sqrt(norm * (norm_of(along) + 1e-06)))
            ratio = guarded(1.0, alpha, 0.1)
            y_second = add(y_first, -alpha, along)
            u_second = image(y_second)
            for part, (y, u_of) in enumerate(((y_first, u_first), (y_second, u_second))):
                resid = add(resid, -alpha, u_of)
                direc = add(y, theta * theta * eta * ratio, direc)
                if part == 1 and n == ITERS:
                    sums = jnp.zeros((8, b), F32)
                    for u, s in members:
                        value = apply_row(solve, (2 * n - 1) % 2, u, s) * resid[2 * n]
                        for i in range(2 * n):
                            value = value + basis[solve, i, at_of(u, s), :] * resid[i]
                        sums = sums + fold(value * value)
                    size = column(sums)
                else:
                    if part == 1:
                        power(2 * n)
                    size = norm_of(resid)
                theta = jnp.sqrt(size) / tau
                cosine = 1.0 / jnp.sqrt(1.0 + theta * theta)
                tau = tau * theta * cosine
                eta = cosine * cosine * alpha
                sol = add(sol, active * eta, direc)

        for u, s in members:
            value = basis[solve, 0, at_of(u, s), :] * sol[0]
            for i in range(1, 2 * ITERS):
                value = value + basis[solve, i, at_of(u, s), :] * sol[i]
            out[rows[solve], 3 * tx(u) + ty(s)] = value

    def between(j):
        if j == 1:
            relay(2)
            near_c0[2].wait_recv()
            start(has_hop, far_c0[2])
            start(has_outer, out_end[0][0])
            near_c1[2].wait_recv()
            start(has_outer, out_end[0][1])
            put_column(2, n_c0, 1, 2, 1)
            put_column(2, n_c1, 1, 2, 0)
        if j == 2:
            arrived(has_far, far_direct[6])
            start(both(has_far, has_outer), out_end[1][1])
            put_column(0, f_c1, 1, 2, 2)
            arrived(has_outer, out_m[0], *out_mid[0])
            arrived(both(has_far, has_outer), out_m[1], *out_mid[1])
            for side in (0, 1):
                widen(10 + side, d_m[1, side])
        if j == 3:
            arrived(has_far, far_c0[2])
            start(both(has_far, has_outer), out_end[1][0])
            put_column(0, f_c0, 1, 2, 1)
            near_r[2].wait_recv()
            start(has_outer, out_r[0])
            put_rhs(1, 1, 2, n_r[rows[1], 1])
        if j == 4:
            arrived(has_far, far_direct[3])
            start(both(has_far, has_outer), out_r[1])
            put_rhs(1, 1, 0, f_r[rows[1], 1])
            arrived(has_far, far_direct[4])
            put_rhs(1, 0, 0, f_r[rows[0], tx(2)])
        if j == 5:
            near_r[3].wait_recv()
            put_rhs(1, 0, 2, n_r[rows[0], tx(2)])
            arrived(has_outer, out_r[0], *out_end[0])
            arrived(both(has_far, has_outer), out_r[1], *out_end[1])
            for side in (0, 1):
                put_corner(1, side, (0, 1))
                put_rhs(1, 2, 2 - 2 * side, d_r[1, side])

    solve_cluster(0, between)
    solve_cluster(1, lambda j: None)

    sent(None, n_mask, *near_c0, *near_c1, *near_r, *direct_in, in_m[0], in_r[0], *in_c[0])
    sent(has_hop, f_mask, *far_c0)
    for i, copy in enumerate(far_direct):
        sent(both(has_far, jnp.logical_not(is_relayed(i))), copy)
    for i, copy in enumerate(far_pass):
        sent(is_relayed(i), copy)
        sent(far_group[i] < partner_relayed, far_hop[i])
    sent(has_outer, *direct_out)
    for side in (0, 1):
        if side:
            sent(has_far, in_m[1], in_r[1], *in_c[1])
        sent(has_outer if side == 0 else both(has_far, has_outer),
             out_m[side], out_r[side], *out_mid[side], *out_end[side])
    assert all(sum(1 for key in numbers if key[0] == kind) <= COPIES for kind in ("send", "recv"))


def shards(blocks, pair_mask, rhs_rows, counts):
    groups = blocks.shape[0]
    b = blocks.shape[-1]
    atoms = pair_mask.shape[-1]
    offsets = pair_mask.shape[2]
    blocks = blocks.reshape(groups, 3, 3, b, b)
    rhs = rhs_rows.reshape(groups, 3, 3, b, b)
    masks = pair_mask.transpose(0, 1, 3, 4, 2).reshape(groups, atoms, atoms, offsets)
    any_spec = pl.BlockSpec(memory_space=pl.ANY)
    vmem_spec = pl.BlockSpec(memory_space=pltpu.VMEM)

    def raw(*lead):
        return pltpu.VMEM(lead + (b, b), F32)

    def flags(*lead):
        return pltpu.VMEM(lead + (atoms, atoms, offsets), jnp.int32)

    solved = pl.pallas_call(
        kernel,
        out_shape=pltpu.VMEM((groups, 9, b, b), F32),
        in_specs=[any_spec, any_spec, any_spec, vmem_spec, vmem_spec],
        out_specs=vmem_spec,
        scratch_shapes=[
            raw(groups, 3, 3), raw(2, 2, 3), raw(groups, 3), raw(groups, 3), raw(groups, 3),
            raw(groups, 3), raw(2, 2, 2, 2), raw(9),
            raw(4), raw(2), raw(groups, 3), raw(groups, 3), raw(2, 2),
            flags(groups), flags(groups), flags(2), flags(2, 2),
            pltpu.VMEM((12, offsets, atoms * b), F32),
            pltpu.VMEM((3, 2 * b, 6 * b), BF16),
            pltpu.VMEM((3, 2 * b, 9 * b), BF16),
            pltpu.VMEM((3, 2 * b, 9 * b), BF16),
            pltpu.VMEM((3, 2 * b, 6 * b), BF16),
            pltpu.VMEM((2, 2, 9 * b, 2 * b), BF16),
            pltpu.VMEM((2, 2 * ITERS, 9 * b, b), F32),
            pltpu.SemaphoreType.DMA((COPIES,)),
            pltpu.SemaphoreType.DMA((COPIES,)),
            pltpu.SemaphoreType.DMA((5,)),
        ],
        compiler_params=pltpu.CompilerParams(
            collective_id=0, has_side_effects=True, vmem_limit_bytes=60 * 1024 * 1024
        ),
    )(blocks, masks, rhs, counts, masks)
    return solved.reshape(groups, 1, 9, b, b)


def solution(mesh):
    spec = P("gx", "gy", None, None, None)
    return jax.shard_map(
        shards,
        mesh=mesh,
        in_specs=(spec, spec, spec, P("gx", "gy", None)),
        out_specs=spec,
        check_vma=False,
    )
```

time: 83.7 us -> 57.6 us (0.69)
  Pallas kernels: 80.5 us -> 56.1 us
  local copies, waits for them, and re-layouts: 2.65 us -> 1.02 us
    pallas_call x1, Pallas kernels: 80.5 us -> 56.1 us  [shards(): pl.pallas_call(kernel, out_shape=pltpu.VMEM((groups, 9, b, b), F32), in_s...]
    unnamed x2 -> x1, local copies, waits for them, and re-layouts: 2.65 us -> 1.02 us
where the time goes in v2:
time: 57.6 us; the launch traced here: 57.1 us
  Pallas kernels  56.1 us (97%)
  local copies, waits for them, and re-layouts  1.02 us (2%)
    pallas_call x1, Pallas kernels, shards(): pl.pallas_call(kernel, out_shape=pltpu.VMEM((groups, 9, b, b), F32), in_s...  56.1 us

profile of v2, /device:TPU:13, one launch (start us, length us, event | category | flops | bytes accessed | tf_op | source)
XLA Modules:
  0.0 57.1 jit_solution(9580958994748733333)
XLA Ops:
  0.0 56.1 %shard_map.46 = f32[2,9,128,128]{3,2,1,0:T(8,128)S(1)} custom-call(f32[2,3,3,128,128]{4,3,2,1,0:T(8,128)} %bitcast.11, s32[2,8,8,9]{3,2,1,0:T(8,128)} %bitcast.13, f32[2,3,3,128,128]{4,3,2,1,0:T(8,128)} %bitcast.12, s32[2,1,8]{2,1,0:T(1,128)} %limits.1, s32[2,8,8,9]{3,2,1,0:T(8,128)} %bitcast.14), custom_call_target="tpu_custom_call" | custom-call | tf_op jit(solution)/shard_map/pallas_call | solution.py:553
  56.1 1.0 %copy.8 = f32[2,1,9,128,128]{4,3,2,1,0:T(8,128)} copy(f32[2,1,9,128,128]{4,3,2,1,0:T(8,128)S(1)} %bitcast.10) | data formatting | bytes 2359296

commit v3 on v2

--- a/solution.py
+++ b/solution.py
@@ -46,9 +46,9 @@
 
 
 def kernel(
-    blocks, masks, rhs, limits, own_masks, out,
+    blocks, masks, rhs, counts, out,
     own_c, g_c, n_c0, n_c1, f_c0, f_c1, d_c, passing,
-    o_r, g_r, n_r, f_r, d_r, n_m, f_m, g_m, d_m, wide,
+    o_r, g_r, n_r, f_r, d_r, own_masks, n_m, f_m, g_m, d_m, limits, wide,
     c_of0, c_of1, c_of2, c_of3, vec, basis,
     send_sem, recv_sem, local_sem,
 ):
@@ -126,8 +126,8 @@
               for i, (row, ous) in enumerate(c_parts)]
     near_r = [remote(rhs.at[row, ous, ty(2)], n_r.at[row, ous], near_dev, ("nr", i))
               for i, (row, ous) in enumerate((
-                  (rows[0], head), (rows[1], pl.ds(tx(0), 1)),
-                  (rows[1], tail), (rows[0], pl.ds(tx(2), 1))))]
+                  (rows[0], head), (rows[1], pl.ds(tx(0), 1)), (rows[1], pl.ds(tx(2), 1)),
+                  (rows[1], pl.ds(1, 1)), (rows[0], pl.ds(tx(2), 1))))]
 
     direct_in = [
         remote(masks.at[rows[0]], g_m.at[0], inner_dev, "gm0"),
@@ -212,7 +212,7 @@
     start(None, *direct_in)
     start(has_outer, *direct_out)
     start_pass(2)
-    start(None, near_c0[2], near_c1[2], near_r[2], near_r[3])
+    start(None, near_c0[2], near_r[2], near_c1[2], near_r[3], near_r[4])
     for i in (6, 3, 4):
         start_direct(i)
 
@@ -220,7 +220,9 @@
     own_rhs = ((0, 1, 0, 1), (0, 2, 1, 0), (1, 0, 0, 2), (1, 1, 1, 1))
     local_r = [pltpu.make_async_copy(rhs.at[rows[t], tx(k), 1], o_r.at[i], local_sem.at[1 + i])
                for i, (_, _, t, k) in enumerate(own_rhs)]
-    start(None, local_c, *local_r)
+    local_m = pltpu.make_async_copy(masks, own_masks, local_sem.at[5])
+    local_n = pltpu.make_async_copy(counts, limits, local_sem.at[6])
+    start(None, local_m, local_c, local_n, *local_r)
 
     def clear(*refs):
         for ref in refs:
@@ -262,9 +264,11 @@
         for part, piece in enumerate(split(value)):
             vec[solve, 0, at:at + b, b * part:b * part + b] = piece
 
-    local_c.wait()
+    local_m.wait()
     for row in (0, 1):
         widen(row, own_masks[row])
+    local_c.wait()
+    local_n.wait()
     for t in (0, 1):
         for k in range(3):
             for j in range(3):
@@ -369,15 +373,42 @@
 
     members = [(u, s) for s in (1, 0, 2) for u in range(3)]
 
-    def apply_row(solve, turn, u, s):
+    def apply_row(solve, turn, u, s, only=(0, 1, 2), low=True):
         found = near_three(s)
+        used = [k for k in found if k in only]
+        if not used:
+            return None
         strips = near_three(u)
-        left = b * len(found) * (strips[0] + solve - first_row[u + solve])
-        width = b * len(found) * len(strips)
-        right = [vec[solve, turn, b * (3 * k + found[0]):b * (3 * k + found[0] + len(found)), :]
+        ref, first = c_refs[u + solve], strips[0] + solve - first_row[u + solve]
+        height = slice(0, 2 * b if low else b)
+        if len(used) == len(found):
+            left = ref[s, height, b * len(found) * first:b * len(found) * (first + len(strips))]
+        else:
+            starts = [b * (len(found) * (first + i) + used[0] - found[0]) for i in range(len(strips))]
+            left = jnp.concatenate(
+                [ref[s, height, at:at + b * len(used)] for at in starts], axis=1)
+        right = [vec[solve, turn, b * (3 * k + used[0]):b * (3 * k + used[0] + len(used)), :]
                  for k in strips]
-        value = product(c_refs[u + solve][s, :, left:left + width], jnp.concatenate(right, axis=0))
-        return value[0:b, 0:b] + (value[0:b, b:2 * b] + value[b:2 * b, 0:b])
+        value = product(left, jnp.concatenate(right, axis=0))
+        total = value[0:b, 0:b] + value[0:b, b:2 * b]
+        return total + value[b:2 * b, 0:b] if low else total
+
+    def before_near(u, s):
+        return () if (u, s) == (2, 2) else (0, 1, 2) if s == 0 else (0, 1)
+
+    def first_product(solve):
+        for u, s in members:
+            value = apply_row(solve, 0, u, s, before_near(u, s))
+            if value is not None:
+                basis[solve, 1, at_of(u, s), :] = value
+
+    def rest_of_first(solve, u, s):
+        done = before_near(u, s)
+        value = apply_row(solve, 0, u, s, tuple(k for k in range(3) if k not in done))
+        if not done:
+            return value
+        partial = basis[solve, 1, at_of(u, s), :]
+        return partial if value is None else partial + value
 
     def solve_cluster(solve, between):
         gram = {}
@@ -385,7 +416,10 @@
         def power(j):
             sums = [jnp.zeros((8, b), F32) for _ in range(j + 1)]
             for u, s in members:
-                value = apply_row(solve, (j - 1) % 2, u, s)
+                if j == 1 and solve == 1:
+                    value = rest_of_first(solve, u, s)
+                else:
+                    value = apply_row(solve, (j - 1) % 2, u, s)
                 basis[solve, j, at_of(u, s), :] = value
                 for part, piece in enumerate(split(value)):
                     vec[solve, j % 2, at_of(u, s), b * part:b * part + b] = piece
@@ -417,10 +451,10 @@
             value = basis[solve, 0, at_of(u, s), :]
             first_sums = first_sums + fold(value * value)
         gram[0, 0] = column(first_sums)
-        counts = limits[rows[solve]].astype(F32)
+        count = limits[rows[solve]].astype(F32)
         atom_of = (lax.broadcasted_iota(jnp.int32, (atoms, b), 1) // orb
                    == lax.broadcasted_iota(jnp.int32, (atoms, b), 0)).astype(F32)
-        limit = product(jnp.broadcast_to(counts, (atoms, atoms)), atom_of)[0:1]
+        limit = product(jnp.broadcast_to(count, (atoms, atoms)), atom_of)[0:1]
 
         power(1)
         norm = gram[0, 0]
@@ -453,7 +487,8 @@
                 if part == 1 and n == ITERS:
                     sums = jnp.zeros((8, b), F32)
                     for u, s in members:
-                        value = apply_row(solve, (2 * n - 1) % 2, u, s) * resid[2 * n]
+                        value = apply_row(solve, (2 * n - 1) % 2, u, s, low=False)
+                        value = value * resid[2 * n]
                         for i in range(2 * n):
                             value = value + basis[solve, i, at_of(u, s), :] * resid[i]
                         sums = sums + fold(value * value)
@@ -480,41 +515,42 @@
             near_c0[2].wait_recv()
             start(has_hop, far_c0[2])
             start(has_outer, out_end[0][0])
-            near_c1[2].wait_recv()
-            start(has_outer, out_end[0][1])
             put_column(2, n_c0, 1, 2, 1)
-            put_column(2, n_c1, 1, 2, 0)
         if j == 2:
-            arrived(has_far, far_direct[6])
-            start(both(has_far, has_outer), out_end[1][1])
-            put_column(0, f_c1, 1, 2, 2)
             arrived(has_outer, out_m[0], *out_mid[0])
             arrived(both(has_far, has_outer), out_m[1], *out_mid[1])
             for side in (0, 1):
                 widen(10 + side, d_m[1, side])
-        if j == 3:
-            arrived(has_far, far_c0[2])
-            start(both(has_far, has_outer), out_end[1][0])
-            put_column(0, f_c0, 1, 2, 1)
             near_r[2].wait_recv()
             start(has_outer, out_r[0])
-            put_rhs(1, 1, 2, n_r[rows[1], 1])
+        if j == 3:
+            arrived(has_far, far_direct[6])
+            start(both(has_far, has_outer), out_end[1][1])
+            put_column(0, f_c1, 1, 2, 2)
         if j == 4:
+            near_c1[2].wait_recv()
+            start(has_outer, out_end[0][1])
+            put_column(2, n_c1, 1, 2, 0)
             arrived(has_far, far_direct[3])
             start(both(has_far, has_outer), out_r[1])
             put_rhs(1, 1, 0, f_r[rows[1], 1])
-            arrived(has_far, far_direct[4])
+        if j == 5:
+            arrived(has_far, far_c0[2], far_direct[4])
+            start(both(has_far, has_outer), out_end[1][0])
+            put_column(0, f_c0, 1, 2, 1)
             put_rhs(1, 0, 0, f_r[rows[0], tx(2)])
-        if j == 5:
-            near_r[3].wait_recv()
-            put_rhs(1, 0, 2, n_r[rows[0], tx(2)])
-            arrived(has_outer, out_r[0], *out_end[0])
-            arrived(both(has_far, has_outer), out_r[1], *out_end[1])
-            for side in (0, 1):
-                put_corner(1, side, (0, 1))
-                put_rhs(1, 2, 2 - 2 * side, d_r[1, side])
 
     solve_cluster(0, between)
+    arrived(both(has_far, has_outer), out_r[1], *out_end[1])
+    put_corner(1, 1, (0, 1))
+    put_rhs(1, 2, 0, d_r[1, 1])
+    first_product(1)
+    arrived(has_outer, out_r[0], *out_end[0])
+    put_corner(1, 0, (0, 1))
+    put_rhs(1, 2, 2, d_r[1, 0])
+    arrived(None, near_r[3], near_r[4])
+    put_rhs(1, 1, 2, n_r[rows[1], 1])
+    put_rhs(1, 0, 2, n_r[rows[0], tx(2)])
     solve_cluster(1, lambda j: None)
 
     sent(None, n_mask, *near_c0, *near_c1, *near_r, *direct_in, in_m[0], in_r[0], *in_c[0])
@@ -553,13 +589,14 @@
     solved = pl.pallas_call(
         kernel,
         out_shape=pltpu.VMEM((groups, 9, b, b), F32),
-        in_specs=[any_spec, any_spec, any_spec, vmem_spec, vmem_spec],
+        in_specs=[any_spec, any_spec, any_spec, any_spec],
         out_specs=vmem_spec,
         scratch_shapes=[
             raw(groups, 3, 3), raw(2, 2, 3), raw(groups, 3), raw(groups, 3), raw(groups, 3),
             raw(groups, 3), raw(2, 2, 2, 2), raw(9),
             raw(4), raw(2), raw(groups, 3), raw(groups, 3), raw(2, 2),
-            flags(groups), flags(groups), flags(2), flags(2, 2),
+            flags(groups), flags(groups), flags(groups), flags(2), flags(2, 2),
+            pltpu.VMEM(counts.shape, jnp.int32),
             pltpu.VMEM((12, offsets, atoms * b), F32),
             pltpu.VMEM((3, 2 * b, 6 * b), BF16),
             pltpu.VMEM((3, 2 * b, 9 * b), BF16),
@@ -569,12 +606,12 @@
             pltpu.VMEM((2, 2 * ITERS, 9 * b, b), F32),
             pltpu.SemaphoreType.DMA((COPIES,)),
             pltpu.SemaphoreType.DMA((COPIES,)),
-            pltpu.SemaphoreType.DMA((5,)),
+            pltpu.SemaphoreType.DMA((7,)),
         ],
         compiler_params=pltpu.CompilerParams(
             collective_id=0, has_side_effects=True, vmem_limit_bytes=60 * 1024 * 1024
         ),
-    )(blocks, masks, rhs, counts, masks)
+    )(blocks, masks, rhs, counts)
     return solved.reshape(groups, 1, 9, b, b)
 
 

time: 57.6 us -> 54.9 us (0.953)
  Pallas kernels: 56.1 us -> 53.7 us
    pallas_call x1, Pallas kernels: 56.1 us -> 53.7 us  [shards(): pl.pallas_call(kernel, out_shape=pltpu.VMEM((groups, 9, b, b), F32), in_s...]
where the time goes in v3:
time: 54.9 us; the launch traced here: 54.7 us
  Pallas kernels  53.7 us (98%)
  local copies, waits for them, and re-layouts  1.02 us (2%)
    pallas_call x1, Pallas kernels, shards(): pl.pallas_call(kernel, out_shape=pltpu.VMEM((groups, 9, b, b), F32), in_s...  53.7 us

profile of v3, /device:TPU:13, one launch (start us, length us, event | category | flops | bytes accessed | tf_op | source)
XLA Modules:
  0.0 54.7 jit_solution(10635514286653524672)
XLA Ops:
  0.0 53.7 %shard_map.46 = f32[2,9,128,128]{3,2,1,0:T(8,128)S(1)} custom-call(f32[2,3,3,128,128]{4,3,2,1,0:T(8,128)} %bitcast.11, s32[2,8,8,9]{3,2,1,0:T(8,128)} %bitcast.13, f32[2,3,3,128,128]{4,3,2,1,0:T(8,128)} %bitcast.12, s32[2,1,8]{2,1,0:T(1,128)} %counts.1), custom_call_target="tpu_custom_call" | custom-call | tf_op jit(solution)/shard_map/pallas_call | solution.py:589
  53.7 1.0 %copy.8 = f32[2,1,9,128,128]{4,3,2,1,0:T(8,128)} copy(f32[2,1,9,128,128]{4,3,2,1,0:T(8,128)S(1)} %bitcast.10) | data formatting | bytes 2359296

commit v4 on v3

--- a/solution.py
+++ b/solution.py
@@ -48,7 +48,7 @@
 def kernel(
     blocks, masks, rhs, counts, out,
     own_c, g_c, n_c0, n_c1, f_c0, f_c1, d_c, passing,
-    o_r, g_r, n_r, f_r, d_r, own_masks, n_m, f_m, g_m, d_m, limits, wide,
+    o_r, g_r, n_r, f_r, d_r, own_masks, own_m, n_m, f_m, g_m, d_m, limits, wide,
     c_of0, c_of1, c_of2, c_of3, vec, basis,
     send_sem, recv_sem, local_sem,
 ):
@@ -99,7 +99,7 @@
             device_id=device, device_id_type=MESH,
         )
 
-    n_mask = remote(masks, n_m, near_dev, "nm")
+    n_mask = remote(own_m, n_m, near_dev, "nm")
     f_mask = remote(n_m, f_m, hop_dev, "fm")
     far_parts = (
         (0, rhs, f_r, rows[0], head, (0, 2)), (0, rhs, f_r, rows[1], pl.ds(tx(0), 1), (2, 1)),
@@ -130,20 +130,20 @@
                   (rows[1], pl.ds(1, 1)), (rows[0], pl.ds(tx(2), 1))))]
 
     direct_in = [
-        remote(masks.at[rows[0]], g_m.at[0], inner_dev, "gm0"),
         remote(rhs.at[rows[0], tx(0), 1], g_r.at[0], inner_dev, "gr0"),
         remote(blocks.at[rows[0], head], g_c.at[0], inner_dev, "gc0"),
+        remote(own_m, g_m.at[0], inner_dev, "gm0"),
     ]
     direct_out = [
-        remote(masks.at[rows[1]], g_m.at[1], outer_dev, "gm1"),
         remote(rhs.at[rows[1], tx(2), 1], g_r.at[1], outer_dev, "gr1"),
         remote(blocks.at[rows[1], tail], g_c.at[1], outer_dev, "gc1"),
+        remote(own_m, g_m.at[1], outer_dev, "gm1"),
     ]
     in_m, in_r, in_c, out_m, out_r, out_mid, out_end = [], [], [], [], [], [], []
     for side, (m, r, coupled) in enumerate(((n_m, n_r, (n_c0, n_c1)), (f_m, f_r, (f_c0, f_c1)))):
-        in_m.append(remote(m.at[rows[0]], d_m.at[0, side], inner_dev, ("im", side)))
+        in_m.append(remote(m, d_m.at[0, side], inner_dev, ("im", side)))
         in_r.append(remote(r.at[rows[0], tx(0)], d_r.at[0, side], inner_dev, ("ir", side)))
-        out_m.append(remote(m.at[rows[1]], d_m.at[1, side], outer_dev, ("om", side)))
+        out_m.append(remote(m, d_m.at[1, side], outer_dev, ("om", side)))
         out_r.append(remote(r.at[rows[1], tx(2)], d_r.at[1, side], outer_dev, ("or", side)))
         in_c.append([remote(c.at[rows[0], head], d_c.at[0, side, k], inner_dev, ("ic", side, k))
                      for k, c in enumerate(coupled)])
@@ -152,6 +152,8 @@
         out_end.append([remote(c.at[rows[1], tx(2)], d_c.at[1, side, k, core], outer_dev, ("oe", side, k))
                         for k, c in enumerate(coupled)])
 
+    local_m = pltpu.make_async_copy(masks, own_masks, local_sem.at[5])
+    local_m.start()
     barrier = pltpu.get_barrier_semaphore()
     total = jnp.int32(0)
     peers = [(inside(gx + step, ngx), (gx + step, gy)) for step in (-1, 1)]
@@ -162,6 +164,16 @@
         @pl.when(exists)
         def _(device=device):
             pl.semaphore_signal(barrier, inc=1, device_id=device, device_id_type=MESH)
+
+    pairs = atoms * atoms
+    local_m.wait()
+    own_m[...] = sum(
+        lax.dot_general(
+            own_masks[row].astype(F32).reshape(pairs, offsets),
+            (lax.broadcasted_iota(jnp.int32, (pairs, 2 * pairs), 0) + pairs * row
+             == lax.broadcasted_iota(jnp.int32, (pairs, 2 * pairs), 1)).astype(F32),
+            (((0,), (0,)), ((), ())), preferred_element_type=F32)
+        for row in (0, 1))
     pl.semaphore_wait(barrier, total)
 
     def on(condition, actions):
@@ -202,9 +214,8 @@
                     copy.wait_recv()
                     far_hop[i].start()
 
-    n_mask.start()
     start_pass(0)
-    start(None, near_c0[0], near_c0[1])
+    start(None, near_c0[0], n_mask, near_c0[1])
     start_pass(1)
     start(None, near_r[0], near_r[1], near_c1[0], near_c1[1])
     for i in (0, 1, 2, 5):
@@ -220,9 +231,8 @@
     own_rhs = ((0, 1, 0, 1), (0, 2, 1, 0), (1, 0, 0, 2), (1, 1, 1, 1))
     local_r = [pltpu.make_async_copy(rhs.at[rows[t], tx(k), 1], o_r.at[i], local_sem.at[1 + i])
                for i, (_, _, t, k) in enumerate(own_rhs)]
-    local_m = pltpu.make_async_copy(masks, own_masks, local_sem.at[5])
     local_n = pltpu.make_async_copy(counts, limits, local_sem.at[6])
-    start(None, local_m, local_c, local_n, *local_r)
+    start(None, local_c, local_n, *local_r)
 
     def clear(*refs):
         for ref in refs:
@@ -236,14 +246,13 @@
     def _():
         clear(g_c.at[1], g_r.at[1], g_m.at[1], d_c.at[1], d_r.at[1], d_m.at[1])
 
-    wide_shape = (atoms * atoms, atoms * b)
+    wide_shape = (pairs, atoms * b)
     above, across = (lax.broadcasted_iota(jnp.int32, wide_shape, d) for d in (0, 1))
     spread = (above == atoms * (across // b) + across % b // orb).astype(F32)
 
-    def widen(index, value):
-        flat = value.astype(F32).reshape(atoms * atoms, offsets)
-        wide[index] = lax.dot_general(
-            flat, spread, (((0,), (0,)), ((), ())), preferred_element_type=F32)
+    def widen(index, packed):
+        for row in (0, 1):
+            wide[index + row] = product(packed[:, pairs * row:pairs * row + pairs], spread)
 
     c_refs = (c_of0, c_of1, c_of2, c_of3)
     first_row = (0, 0, 1, 2)
@@ -264,9 +273,7 @@
         for part, piece in enumerate(split(value)):
             vec[solve, 0, at:at + b, b * part:b * part + b] = piece
 
-    local_m.wait()
-    for row in (0, 1):
-        widen(row, own_masks[row])
+    widen(0, own_m[...])
     local_c.wait()
     local_n.wait()
     for t in (0, 1):
@@ -278,10 +285,10 @@
         put_rhs(solve, u, 1, o_r[i])
 
     arrived(None, *direct_in)
-    widen(2, g_m[0])
+    widen(6, g_m[0])
     for k, slot in ((1, 1 - core), (2, core)):
         for j in range(3):
-            put(0, 1, k, j, g_c[0, slot, ty(j)], 2)
+            put(0, 1, k, j, g_c[0, slot, ty(j)], 6 + core)
     put_rhs(0, 0, 1, g_r[0])
 
     n_mask.wait_recv()
@@ -289,11 +296,10 @@
     start(None, in_m[0])
     start(has_outer, out_m[0])
     relay(0)
-    for row in (0, 1):
-        widen(4 + row, n_m[row])
+    widen(2, n_m[...])
 
     def put_column(s, ref, t, k, j):
-        put(1 + t, s, k, j, ref[rows[t], tx(k)], (4 if s == 2 else 6) + rows[t])
+        put(1 + t, s, k, j, ref[rows[t], tx(k)], (2 if s == 2 else 4) + rows[t])
 
     near_c0[0].wait_recv()
     start(has_hop, far_c0[0])
@@ -314,8 +320,7 @@
     arrived(has_far, f_mask)
     start(has_far, in_m[1])
     start(both(has_far, has_outer), out_m[1])
-    for row in (0, 1):
-        widen(6 + row, f_m[row])
+    widen(4, f_m[...])
     arrived(has_far, far_direct[0], far_direct[1])
     start(has_far, in_r[1])
     put_rhs(0, 1, 0, f_r[rows[0], 1])
@@ -335,10 +340,10 @@
             put_column(0, f_c0, t, k, 1)
 
     arrived(has_outer, *direct_out)
-    widen(3, g_m[1])
+    widen(8, g_m[1])
     for k, slot in ((1, core), (0, 1 - core)):
         for j in range(3):
-            put(3, 1, k, j, g_c[1, slot, ty(j)], 3)
+            put(3, 1, k, j, g_c[1, slot, ty(j)], 9 - core)
     put_rhs(1, 2, 1, g_r[1])
 
     near_c1[0].wait_recv()
@@ -354,11 +359,11 @@
         for way in ways:
             for k, slot in (((1, 1 - core), (2, core)), ((1, core), (0, 1 - core)))[x]:
                 put(3 * x, s, k, 1 if way == 0 else 2 * side, d_c[x, side, way, slot],
-                    8 + 2 * x + side)
+                    10 + 2 * (2 * x + side) + (1 - core if x else core))
 
     for side in (1, 0):
         arrived(side_there[side], in_m[side], in_r[side], *in_c[side])
-        widen(8 + side, d_m[0, side])
+        widen(10 + 2 * side, d_m[0, side])
         put_corner(0, side, (0, 1))
         put_rhs(0, 0, 2 - 2 * side, d_r[0, side])
 
@@ -371,7 +376,7 @@
     def at_of(u, s):
         return slice(b * (3 * u + s), b * (3 * u + s) + b)
 
-    members = [(u, s) for s in (1, 0, 2) for u in range(3)]
+    members = [(u, s) for u in range(3) for s in range(3)]
 
     def apply_row(solve, turn, u, s, only=(0, 1, 2), low=True):
         found = near_three(s)
@@ -520,7 +525,7 @@
             arrived(has_outer, out_m[0], *out_mid[0])
             arrived(both(has_far, has_outer), out_m[1], *out_mid[1])
             for side in (0, 1):
-                widen(10 + side, d_m[1, side])
+                widen(14 + 2 * side, d_m[1, side])
             near_r[2].wait_recv()
             start(has_outer, out_r[0])
         if j == 3:
@@ -584,7 +589,7 @@
         return pltpu.VMEM(lead + (b, b), F32)
 
     def flags(*lead):
-        return pltpu.VMEM(lead + (atoms, atoms, offsets), jnp.int32)
+        return pltpu.VMEM(lead + (offsets, groups * atoms * atoms), F32)
 
     solved = pl.pallas_call(
         kernel,
@@ -595,9 +600,10 @@
             raw(groups, 3, 3), raw(2, 2, 3), raw(groups, 3), raw(groups, 3), raw(groups, 3),
             raw(groups, 3), raw(2, 2, 2, 2), raw(9),
             raw(4), raw(2), raw(groups, 3), raw(groups, 3), raw(2, 2),
-            flags(groups), flags(groups), flags(groups), flags(2), flags(2, 2),
+            pltpu.VMEM((groups, atoms, atoms, offsets), jnp.int32),
+            flags(), flags(), flags(), flags(2), flags(2, 2),
             pltpu.VMEM(counts.shape, jnp.int32),
-            pltpu.VMEM((12, offsets, atoms * b), F32),
+            pltpu.VMEM((18, offsets, atoms * b), F32),
             pltpu.VMEM((3, 2 * b, 6 * b), BF16),
             pltpu.VMEM((3, 2 * b, 9 * b), BF16),
             pltpu.VMEM((3, 2 * b, 9 * b), BF16),

time: 54.9 us -> 53.5 us (0.974)
  Pallas kernels: 53.7 us -> 52.3 us
    pallas_call x1, Pallas kernels: 53.7 us -> 52.3 us  [shards(): pl.pallas_call(kernel, out_shape=pltpu.VMEM((groups, 9, b, b), F32), in_s...]
where the time goes in v4:
time: 53.5 us; the launch traced here: 53.3 us
  Pallas kernels  52.3 us (98%)
  local copies, waits for them, and re-layouts  1.02 us (2%)
    pallas_call x1, Pallas kernels, shards(): pl.pallas_call(kernel, out_shape=pltpu.VMEM((groups, 9, b, b), F32), in_s...  52.3 us

profile of v4, /device:TPU:13, one launch (start us, length us, event | category | flops | bytes accessed | tf_op | source)
XLA Modules:
  0.0 53.3 jit_solution(17123389251806210547)
XLA Ops:
  0.0 52.3 %shard_map.46 = f32[2,9,128,128]{3,2,1,0:T(8,128)S(1)} custom-call(f32[2,3,3,128,128]{4,3,2,1,0:T(8,128)} %bitcast.11, s32[2,8,8,9]{3,2,1,0:T(8,128)} %bitcast.13, f32[2,3,3,128,128]{4,3,2,1,0:T(8,128)} %bitcast.12, s32[2,1,8]{2,1,0:T(1,128)} %counts.1), custom_call_target="tpu_custom_call" | custom-call | tf_op jit(solution)/shard_map/pallas_call | solution.py:594
  52.3 1.0 %copy.8 = f32[2,1,9,128,128]{4,3,2,1,0:T(8,128)} copy(f32[2,1,9,128,128]{4,3,2,1,0:T(8,128)S(1)} %bitcast.10) | data formatting | bytes 2359296

commit v5 on v4

--- a/solution.py
+++ b/solution.py
@@ -10,6 +10,10 @@
 MESH = pl.DeviceIdType.MESH
 F32 = jnp.float32
 BF16 = jnp.bfloat16
+E4M3 = jnp.float8_e4m3fn
+E5M2 = jnp.float8_e5m2
+C_SCALE = 2.0 ** 21
+V_SCALE = 2.0 ** 5
 
 
 def guarded(top, bottom, floor_val):
@@ -49,7 +53,7 @@
     blocks, masks, rhs, counts, out,
     own_c, g_c, n_c0, n_c1, f_c0, f_c1, d_c, passing,
     o_r, g_r, n_r, f_r, d_r, own_masks, own_m, n_m, f_m, g_m, d_m, limits, wide,
-    c_of0, c_of1, c_of2, c_of3, vec, basis,
+    c_of0, c_of1, c_of2, c_of3, r_of0, r_of1, r_of2, r_of3, vec, coarse, basis,
     send_sem, recv_sem, local_sem,
 ):
     b = blocks.shape[-1]
@@ -101,11 +105,13 @@
 
     n_mask = remote(own_m, n_m, near_dev, "nm")
     f_mask = remote(n_m, f_m, hop_dev, "fm")
+    low_end, high_end, middle = pl.ds(tx(0), 1), pl.ds(tx(2), 1), pl.ds(1, 1)
     far_parts = (
-        (0, rhs, f_r, rows[0], head, (0, 2)), (0, rhs, f_r, rows[1], pl.ds(tx(0), 1), (2, 1)),
-        (1, blocks, f_c1, rows[0], full, (3, 3)),
-        (2, rhs, f_r, rows[1], tail, (6, 2)), (2, rhs, f_r, rows[0], pl.ds(tx(2), 1), (8, 1)),
-        (4, blocks, f_c1, rows[1], head, None), (4, blocks, f_c1, rows[1], pl.ds(tx(2), 1), None),
+        (0, rhs, f_r, rows[0], head, (0, 2)), (0, blocks, f_c1, rows[1], high_end, (2, 1)),
+        (1, blocks, f_c1, rows[1], head, (3, 2)), (1, rhs, f_r, rows[0], high_end, (5, 1)),
+        (2, blocks, f_c1, rows[0], head, (6, 2)), (2, rhs, f_r, rows[1], high_end, (8, 1)),
+        (4, blocks, f_c1, rows[0], high_end, None), (4, rhs, f_r, rows[1], low_end, None),
+        (4, rhs, f_r, rows[1], middle, None),
     )
     far_direct, far_pass, far_hop, far_group = [], [], [], []
     for i, (group, source, target, row, ous, slot) in enumerate(far_parts):
@@ -198,33 +204,31 @@
     def is_relayed(i):
         return far_group[i] < mine_relayed
 
-    def start_pass(group):
-        for i, copy in enumerate(far_pass):
-            if far_group[i] == group:
-                start(is_relayed(i), copy)
+    def start_pass(*items):
+        for i in items:
+            start(is_relayed(i), far_pass[i])
 
     def start_direct(i):
         start(both(has_far, jnp.logical_not(is_relayed(i))), far_direct[i])
 
-    def relay(group):
-        for i, copy in enumerate(far_pass):
-            if far_group[i] == group:
-                @pl.when(group < partner_relayed)
-                def _(i=i, copy=copy):
-                    copy.wait_recv()
-                    far_hop[i].start()
+    def relay(*items):
+        for i in items:
+            @pl.when(far_group[i] < partner_relayed)
+            def _(i=i):
+                far_pass[i].wait_recv()
+                far_hop[i].start()
 
     start_pass(0)
     start(None, near_c0[0], n_mask, near_c0[1])
-    start_pass(1)
+    start_pass(2, 4)
     start(None, near_r[0], near_r[1], near_c1[0], near_c1[1])
-    for i in (0, 1, 2, 5):
+    for i in (0, 7, 4, 6, 2):
         start_direct(i)
     start(None, *direct_in)
     start(has_outer, *direct_out)
-    start_pass(2)
+    start_pass(1, 5, 3)
     start(None, near_c0[2], near_r[2], near_c1[2], near_r[3], near_r[4])
-    for i in (6, 3, 4):
+    for i in (1, 5, 8, 3):
         start_direct(i)
 
     local_c = pltpu.make_async_copy(blocks, own_c, local_sem.at[0])
@@ -255,17 +259,21 @@
             wide[index + row] = product(packed[:, pairs * row:pairs * row + pairs], spread)
 
     c_refs = (c_of0, c_of1, c_of2, c_of3)
+    r_refs = (r_of0, r_of1, r_of2, r_of3)
     first_row = (0, 0, 1, 2)
 
     def put(w, s, k, j, value, mask):
         mask_row = wide[mask, pl.ds(3 * tx(k) + ty(j), 1), :]
         found = near_three(s)
         col = b * ((w + k - 1 - first_row[w]) * len(found) + s + j - 1 - found[0])
-        for i in range(atoms):
-            masked = value[orb * i:orb * (i + 1)] * mask_row[:, b * i:b * (i + 1)]
-            for part, piece in enumerate(split(masked)):
-                at = b * part + orb * i
-                c_refs[w][s, at:at + orb, col:col + b] = piece
+        masked = jnp.concatenate(
+            [value[orb * i:orb * (i + 1)] * mask_row[:, b * i:b * (i + 1)] for i in range(atoms)],
+            axis=0)
+        high = masked.astype(BF16)
+        rest = masked - high.astype(F32)
+        c_refs[w][s, 0:b, col:col + b] = high
+        c_refs[w][s, b:2 * b, col:col + b] = rest.astype(BF16)
+        r_refs[w][s, :, col:col + b] = (rest * C_SCALE).astype(E4M3)
 
     def put_rhs(solve, u, s, value):
         at = b * (3 * u + s)
@@ -311,7 +319,7 @@
     start(has_outer, out_mid[0][0])
     for k in (0, 1):
         put_column(2, n_c0, 1, k, 1)
-    relay(1)
+    relay(2, 4)
     arrived(None, near_r[0], near_r[1])
     start(None, in_r[0])
     put_rhs(0, 1, 2, n_r[rows[0], 1])
@@ -321,13 +329,13 @@
     start(has_far, in_m[1])
     start(both(has_far, has_outer), out_m[1])
     widen(4, f_m[...])
-    arrived(has_far, far_direct[0], far_direct[1])
+    arrived(has_far, far_direct[0], far_direct[7])
     start(has_far, in_r[1])
     put_rhs(0, 1, 0, f_r[rows[0], 1])
     put_rhs(0, 2, 0, f_r[rows[1], tx(0)])
-    arrived(has_far, far_direct[2])
+    arrived(has_far, far_direct[4])
     start(has_far, in_c[1][1])
-    arrived(has_far, far_direct[5])
+    arrived(has_far, far_direct[6], far_direct[2])
     start(both(has_far, has_outer), out_mid[1][1])
     for t, ks in ((0, (0, 1, 2)), (1, (0, 1))):
         for k in ks:
@@ -378,7 +386,7 @@
 
     members = [(u, s) for u in range(3) for s in range(3)]
 
-    def apply_row(solve, turn, u, s, only=(0, 1, 2), low=True):
+    def apply_row(solve, turn, u, s, only=(0, 1, 2), low=True, scale=None):
         found = near_three(s)
         used = [k for k in found if k in only]
         if not used:
@@ -396,6 +404,12 @@
                  for k in strips]
         value = product(left, jnp.concatenate(right, axis=0))
         total = value[0:b, 0:b] + value[0:b, b:2 * b]
+        if scale is not None:
+            lanes = slice(b * len(found) * first, b * len(found) * (first + len(strips)))
+            right = [coarse[solve, turn, b * (3 * k + found[0]):b * (3 * k + found[0] + len(found)), :]
+                     for k in strips]
+            return total + scale * product(
+                r_refs[u + solve][s, :, lanes], jnp.concatenate(right, axis=0))
         return total + value[b:2 * b, 0:b] if low else total
 
     def before_near(u, s):
@@ -417,15 +431,23 @@
 
     def solve_cluster(solve, between):
         gram = {}
+        lengths = {}
 
         def power(j):
+            square = gram[j - 1, j - 1]
+            inverse = jnp.where(square > 0.0, lax.rsqrt(square), 0.0)
+            lengths[j - 1] = square * inverse
+            shrink = V_SCALE * inverse
             sums = [jnp.zeros((8, b), F32) for _ in range(j + 1)]
             for u, s in members:
                 if j == 1 and solve == 1:
                     value = rest_of_first(solve, u, s)
                 else:
-                    value = apply_row(solve, (j - 1) % 2, u, s)
+                    scale = None if j == 1 else lengths[j - 2] * (1.0 / (C_SCALE * V_SCALE))
+                    value = apply_row(solve, (j - 1) % 2, u, s, low=j == 1, scale=scale)
                 basis[solve, j, at_of(u, s), :] = value
+                if j < 2 * ITERS - 1:
+                    coarse[solve, j % 2, at_of(u, s), :] = (value * shrink).astype(E5M2)
                 for part, piece in enumerate(split(value)):
                     vec[solve, j % 2, at_of(u, s), b * part:b * part + b] = piece
                 for i in range(j):
@@ -516,7 +538,7 @@
 
     def between(j):
         if j == 1:
-            relay(2)
+            relay(1, 5, 3)
             near_c0[2].wait_recv()
             start(has_hop, far_c0[2])
             start(has_outer, out_end[0][0])
@@ -529,18 +551,18 @@
             near_r[2].wait_recv()
             start(has_outer, out_r[0])
         if j == 3:
-            arrived(has_far, far_direct[6])
+            arrived(has_far, far_direct[1])
             start(both(has_far, has_outer), out_end[1][1])
             put_column(0, f_c1, 1, 2, 2)
         if j == 4:
             near_c1[2].wait_recv()
             start(has_outer, out_end[0][1])
             put_column(2, n_c1, 1, 2, 0)
-            arrived(has_far, far_direct[3])
+            arrived(has_far, far_direct[5], far_direct[8])
             start(both(has_far, has_outer), out_r[1])
             put_rhs(1, 1, 0, f_r[rows[1], 1])
         if j == 5:
-            arrived(has_far, far_c0[2], far_direct[4])
+            arrived(has_far, far_c0[2], far_direct[3])
             start(both(has_far, has_outer), out_end[1][0])
             put_column(0, f_c0, 1, 2, 1)
             put_rhs(1, 0, 0, f_r[rows[0], tx(2)])
@@ -608,7 +630,12 @@
             pltpu.VMEM((3, 2 * b, 9 * b), BF16),
             pltpu.VMEM((3, 2 * b, 9 * b), BF16),
             pltpu.VMEM((3, 2 * b, 6 * b), BF16),
+            pltpu.VMEM((3, b, 6 * b), E4M3),
+            pltpu.VMEM((3, b, 9 * b), E4M3),
+            pltpu.VMEM((3, b, 9 * b), E4M3),
+            pltpu.VMEM((3, b, 6 * b), E4M3),
             pltpu.VMEM((2, 2, 9 * b, 2 * b), BF16),
+            pltpu.VMEM((2, 2, 9 * b, b), E5M2),
             pltpu.VMEM((2, 2 * ITERS, 9 * b, b), F32),
             pltpu.SemaphoreType.DMA((COPIES,)),
             pltpu.SemaphoreType.DMA((COPIES,)),

time: 53.5 us -> 53.2 us (level)
  Pallas kernels: 52.3 us -> 51.7 us
    pallas_call x1, Pallas kernels: 52.3 us -> 51.7 us  [shards(): pl.pallas_call(kernel, out_shape=pltpu.VMEM((groups, 9, b, b), F32), in_s...]
where the time goes in v5:
time: 53.2 us; the launch traced here: 52.8 us
  Pallas kernels  51.7 us (97%)
  local copies, waits for them, and re-layouts  1.02 us (2%)
    pallas_call x1, Pallas kernels, shards(): pl.pallas_call(kernel, out_shape=pltpu.VMEM((groups, 9, b, b), F32), in_s...  51.7 us

profile of v5, /device:TPU:13, one launch (start us, length us, event | category | flops | bytes accessed | tf_op | source)
XLA Modules:
  0.0 52.8 jit_solution(2833982696674689606)
XLA Ops:
  0.0 51.7 %shard_map.46 = f32[2,9,128,128]{3,2,1,0:T(8,128)S(1)} custom-call(f32[2,3,3,128,128]{4,3,2,1,0:T(8,128)} %bitcast.11, s32[2,8,8,9]{3,2,1,0:T(8,128)} %bitcast.13, f32[2,3,3,128,128]{4,3,2,1,0:T(8,128)} %bitcast.12, s32[2,1,8]{2,1,0:T(1,128)} %counts.1), custom_call_target="tpu_custom_call" | custom-call | tf_op jit(solution)/shard_map/pallas_call | solution.py:616
  51.7 1.0 %copy.8 = f32[2,1,9,128,128]{4,3,2,1,0:T(8,128)} copy(f32[2,1,9,128,128]{4,3,2,1,0:T(8,128)S(1)} %bitcast.10) | data formatting | bytes 2359296

commit v6 on v5

--- a/solution.py
+++ b/solution.py
@@ -76,7 +76,6 @@
     has_outer = inside(gx - step_x, ngx)
     has_far = inside(gy - step_y, ngy)
     has_hop = inside(gy + 2 * step_y, ngy)
-    side_there = (None, has_far)
     rank = jnp.where(odd == 0, gy // 2, half - 1 - gy // 2)
     mine_relayed = (4 * rank) // half
     partner_relayed = (4 * (half - 1 - rank)) // half
@@ -354,26 +353,12 @@
             put(3, 1, k, j, g_c[1, slot, ty(j)], 9 - core)
     put_rhs(1, 2, 1, g_r[1])
 
-    near_c1[0].wait_recv()
-    start(None, in_c[0][1])
-    near_c1[1].wait_recv()
-    start(has_outer, out_mid[0][1])
-    for t, ks in ((0, (0, 1, 2)), (1, (0, 1))):
-        for k in ks:
-            put_column(2, n_c1, t, k, 0)
-
     def put_corner(x, side, ways):
         s = 2 - 2 * side
         for way in ways:
             for k, slot in (((1, 1 - core), (2, core)), ((1, core), (0, 1 - core)))[x]:
                 put(3 * x, s, k, 1 if way == 0 else 2 * side, d_c[x, side, way, slot],
                     10 + 2 * (2 * x + side) + (1 - core if x else core))
-
-    for side in (1, 0):
-        arrived(side_there[side], in_m[side], in_r[side], *in_c[side])
-        widen(10 + 2 * side, d_m[0, side])
-        put_corner(0, side, (0, 1))
-        put_rhs(0, 0, 2 - 2 * side, d_r[0, side])
 
     def fold(value):
         return jnp.sum(value.reshape(-1, 8, b), axis=0)
@@ -412,17 +397,19 @@
                 r_refs[u + solve][s, :, lanes], jnp.concatenate(right, axis=0))
         return total + value[b:2 * b, 0:b] if low else total
 
-    def before_near(u, s):
+    def before_near(solve, u, s):
+        if solve == 0:
+            return () if s == 2 else (0, 1, 2)
         return () if (u, s) == (2, 2) else (0, 1, 2) if s == 0 else (0, 1)
 
     def first_product(solve):
         for u, s in members:
-            value = apply_row(solve, 0, u, s, before_near(u, s))
+            value = apply_row(solve, 0, u, s, before_near(solve, u, s))
             if value is not None:
                 basis[solve, 1, at_of(u, s), :] = value
 
     def rest_of_first(solve, u, s):
-        done = before_near(u, s)
+        done = before_near(solve, u, s)
         value = apply_row(solve, 0, u, s, tuple(k for k in range(3) if k not in done))
         if not done:
             return value
@@ -440,11 +427,11 @@
             shrink = V_SCALE * inverse
             sums = [jnp.zeros((8, b), F32) for _ in range(j + 1)]
             for u, s in members:
-                if j == 1 and solve == 1:
+                if j == 1:
                     value = rest_of_first(solve, u, s)
                 else:
-                    scale = None if j == 1 else lengths[j - 2] * (1.0 / (C_SCALE * V_SCALE))
-                    value = apply_row(solve, (j - 1) % 2, u, s, low=j == 1, scale=scale)
+                    scale = lengths[j - 2] * (1.0 / (C_SCALE * V_SCALE))
+                    value = apply_row(solve, (j - 1) % 2, u, s, low=False, scale=scale)
                 basis[solve, j, at_of(u, s), :] = value
                 if j < 2 * ITERS - 1:
                     coarse[solve, j % 2, at_of(u, s), :] = (value * shrink).astype(E5M2)
@@ -567,6 +554,23 @@
             put_column(0, f_c0, 1, 2, 1)
             put_rhs(1, 0, 0, f_r[rows[0], tx(2)])
 
+    arrived(has_far, in_m[1], in_r[1], *in_c[1])
+    widen(12, d_m[0, 1])
+    put_corner(0, 1, (0, 1))
+    put_rhs(0, 0, 0, d_r[0, 1])
+    arrived(None, in_m[0], in_r[0])
+    widen(10, d_m[0, 0])
+    put_rhs(0, 0, 2, d_r[0, 0])
+    near_c1[0].wait_recv()
+    start(None, in_c[0][1])
+    first_product(0)
+    near_c1[1].wait_recv()
+    start(has_outer, out_mid[0][1])
+    for t, ks in ((0, (0, 1, 2)), (1, (0, 1))):
+        for k in ks:
+            put_column(2, n_c1, t, k, 0)
+    arrived(None, *in_c[0])
+    put_corner(0, 0, (0, 1))
     solve_cluster(0, between)
     arrived(both(has_far, has_outer), out_r[1], *out_end[1])
     put_corner(1, 1, (0, 1))

time: 53.2 us -> 53 us (level)
  no operation moved by 1% of the time
where the time goes in v6:
time: 53 us; the launch traced here: 52.8 us
  Pallas kernels  51.8 us (98%)
  local copies, waits for them, and re-layouts  1.02 us (2%)
    pallas_call x1, Pallas kernels, shards(): pl.pallas_call(kernel, out_shape=pltpu.VMEM((groups, 9, b, b), F32), in_s...  51.8 us

profile of v6, /device:TPU:13, one launch (start us, length us, event | category | flops | bytes accessed | tf_op | source)
XLA Modules:
  0.0 52.8 jit_solution(13575418950529889674)
XLA Ops:
  0.0 51.8 %shard_map.46 = f32[2,9,128,128]{3,2,1,0:T(8,128)S(1)} custom-call(f32[2,3,3,128,128]{4,3,2,1,0:T(8,128)} %bitcast.11, s32[2,8,8,9]{3,2,1,0:T(8,128)} %bitcast.13, f32[2,3,3,128,128]{4,3,2,1,0:T(8,128)} %bitcast.12, s32[2,1,8]{2,1,0:T(1,128)} %counts.1), custom_call_target="tpu_custom_call" | custom-call | tf_op jit(solution)/shard_map/pallas_call | solution.py:620
  51.8 1.0 %copy.8 = f32[2,1,9,128,128]{4,3,2,1,0:T(8,128)} copy(f32[2,1,9,128,128]{4,3,2,1,0:T(8,128)S(1)} %bitcast.10) | data formatting | bytes 2359296
